TPU v7x, 32 devices: a whole 2x2x4 slice. The times are simulated.
32 devices in a mesh: cons: 4 (over y, core), prod: 8 (over z, x).
Axes of the slice: x: 2, y: 2, z: 4, core: 2. Of those that a mesh axis runs over, the one named last changes fastest.
Arguments:
- tastes: bfloat16 [16384, 128], P('cons'), may hold values from -128 to 128
- price_coef: float32 [16384], P('cons'), may hold values from 0.5 to 5
- characteristics: bfloat16 [16384, 128], P('prod'), may hold values from -6 to 6
- mean_utility: float32 [16384], P('prod'), may hold values from -4 to 4
- panel_cols: int32 [256], replicated, may hold values from 0 to 16383
- firm_map: int32 [16384], P('prod'), may hold values from 0 to 16383, as said below
- inverses: float32 [128, 128, 128], P('prod'), may hold values from -0.5 to 0.5
Outputs:
- shares: float32 [16384], P('prod')
- markup: float32 [16384], P('prod')
- response: float32 [16384, 256], P('prod')
Inputs may be any that keep to these rules, and one draw needn't show every extreme that they name: `firm_map`: a permutation of the products; the rows of firm order held by each index of prod name exactly 256 products held by each index of prod.
All inputs are finite; a program needn't handle non-finite values.
Results may differ from a plain program's by a relative error of at most 0.002.
The roundings to bfloat16 on the way count: a program that leaves them out, or rounds other values in their place, can miss the bound.
Values may be sent and summed in bfloat16 or wider, within the bound.
A program may use at most 64 MiB of HBM per device.

v0:
```python
import functools
import jax
import jax.numpy as jnp
from jax import lax
from jax.experimental import pallas as pl
from jax.experimental.pallas import tpu as pltpu
from jax.sharding import PartitionSpec as P

F32 = jnp.float32
BF16 = jnp.bfloat16
NT = (((1,), (1,)), ((), ()))
MESH = pl.DeviceIdType.MESH
VMEM = pl.BlockSpec(memory_space=pltpu.VMEM)
LIMIT = 63 * 1024 * 1024


def turned(row):
    return jnp.broadcast_to(row, (128, 128)).T


def prep_kernel(
    n, LP, cp,
    sid, fm, chars, mean, cols,
    C, colpart, colmean, asked,
    CA, X, XM, XC, XCM, R, RM, RC, RCM,
    a_s, a_r, x_s, x_r, f_s, f_r, m_s, m_r, c_s, c_r, k_s, k_r,
):
    me = lax.axis_index("prod")
    cons = lax.axis_index("cons")
    core = lax.rem(cons, 2)
    partner = cons + 1 - 2 * core
    K = chars.shape[1]
    pad = sid.shape[2]
    base = me * LP
    barrier = pltpu.get_barrier_semaphore()
    for d in range(1, n):
        pl.semaphore_signal(barrier, inc=1, device_id={"prod": lax.rem(me + d, n)}, device_id_type=MESH)
    pl.semaphore_signal(barrier, inc=1, device_id={"cons": partner}, device_id_type=MESH)

    CA[:, :K] = chars[...]
    lane = lax.broadcasted_iota(jnp.int32, (128, K), 1)

    def split(column):
        a = column.astype(BF16).astype(F32)
        b = (column - a).astype(BF16).astype(F32)
        c = column - a - b
        return jnp.where(lane == 0, a, jnp.where(lane == 1, b, jnp.where(lane == 2, c, 0.0))).astype(BF16)

    def widen(g, carry):
        rows = pl.ds(pl.multiple_of(g * 128, 128), 128)
        CA[rows, K:] = split(turned(mean[:, rows]))
        return carry

    lax.fori_loop(0, LP // 128, widen, 0)
    pl.semaphore_wait(barrier, n)

    def send(src, dst, s, r, d):
        return pltpu.make_async_remote_copy(
            src, dst, s.at[d], r.at[d],
            device_id={"prod": lax.rem(me + d, n)}, device_id_type=MESH,
        )

    span = pad // 2
    part = pl.ds(pl.multiple_of(core * span, span), span)

    def a_copy(d):
        return send(sid.at[lax.rem(me + d, n)], asked.at[me], a_s, a_r, d)

    def x_copy(d):
        return send(X.at[lax.rem(me + d, n), part], R.at[me, part], x_s, x_r, d)

    def m_copy(d):
        return send(XM.at[lax.rem(me + d, n)], RM.at[me], m_s, m_r, d)

    def c_copy(d):
        return send(XC.at[lax.rem(me + d, n)], RC.at[me], c_s, c_r, d)

    def k_copy(d):
        return send(XCM, RCM.at[me], k_s, k_r, d)

    def f_copy(d):
        source = lax.rem(me + n - d, n)
        return pltpu.make_async_remote_copy(
            R.at[source, part], R.at[source, part], f_s.at[d], f_r.at[d],
            device_id={"cons": partner}, device_id_type=MESH,
        )

    def loop(fn, lo=1):
        def step(d, carry):
            fn(d)
            return carry
        lax.fori_loop(lo, n, step, 0)

    loop(lambda d: a_copy(d).start())
    asked[me] = sid[me]

    def pick(row):
        want = turned((row - base).astype(F32))
        spot = lax.broadcasted_iota(jnp.int32, (128, 128), 1).astype(F32)
        hot = jnp.concatenate(
            [jnp.where(want == spot + float(b * 128), 1.0, 0.0).astype(BF16) for b in range(LP // 128)], axis=1
        )
        got = jnp.dot(hot, CA[...], preferred_element_type=F32)
        t = got[:, K:].T
        return got[:, :K], t[0:1] + (t[1:2] + t[2:3])

    for g in range(cols.shape[1] // 128):
        at = pl.ds(g * 128, 128)
        rows, means = pick(cols[:, at])
        lots = 128 // cp
        XC[g * lots:(g + 1) * lots, :cp, :] = rows.reshape(lots, cp, K).astype(BF16)
        XCM[:, at] = means
    loop(lambda d: c_copy(d).start())
    loop(lambda d: k_copy(d).start())
    RC[me] = XC[me]
    RCM[me] = XCM[...]

    def answer(d, carry):
        source = lax.rem(me + n - d, n)

        @pl.when(d > 0)
        def _():
            send(sid.at[source], asked.at[source], a_s, a_r, lax.rem(n - d, n)).wait_send()
            send(sid.at[source], asked.at[source], a_s, a_r, d).wait_recv()

        for b in range(pad // 128):
            at = pl.ds(b * 128, 128)
            rows, means = pick(asked[source, :, at])
            X[source, at, :] = rows.astype(BF16)
            XM[source, :, at] = means

        @pl.when(d > 0)
        def _():
            back = lax.rem(n - d, n)
            x_copy(back).start()
            m_copy(back).start()

        return carry

    lax.fori_loop(0, n, answer, 0)
    R[me] = X[me]
    RM[me] = XM[me]

    loop(lambda d: c_copy(d).wait())
    loop(lambda d: k_copy(d).wait())
    total = RC[0, :cp, :].astype(F32)
    heads = RCM[0]
    for p in range(1, n):
        total = total + RC[p, :cp, :].astype(F32)
        heads = heads + RCM[p]
    colpart[...] = total
    colmean[...] = heads

    def relay(d):
        x_copy(d).wait()
        f_copy(d).start()

    loop(relay)
    loop(lambda d: m_copy(d).wait())
    loop(lambda d: f_copy(d).wait())
    table = R[...].reshape(n * pad, K)

    def firm(g, carry):
        bands = []
        for h in range(2):
            rows = pl.ds(pl.multiple_of(g * 256 + h * 128, 128), 128)
            want = turned(fm[:, rows].astype(F32))
            hots = []
            mid = jnp.zeros((128, 128), F32)
            for p in range(n):
                for b in range(pad // 128):
                    at = pl.ds(b * 128, 128)
                    hit = want == sid[p, :, at].astype(F32)
                    hots.append(jnp.where(hit, 1.0, 0.0).astype(BF16))
                    mid = mid + jnp.where(hit, RM[p, :, at], 0.0)
            bands.append(jnp.concatenate(hots, axis=1))
            C[rows, K:] = split(jnp.sum(mid, axis=1, keepdims=True))
        rows = pl.ds(pl.multiple_of(g * 256, 256), 256)
        C[rows, :K] = jnp.dot(jnp.concatenate(bands, axis=0), table, preferred_element_type=F32).astype(BF16)
        return carry

    lax.fori_loop(0, LP // 256, firm, 0)


def prepare(n, sid, fm, chars, mean, cols):
    LP, K = chars.shape
    W = cols.shape[1]
    cp = W // n
    room = -(-cp // 16) * 16
    pad = sid.shape[2]
    dma = pltpu.SemaphoreType.DMA
    return pl.pallas_call(
        functools.partial(prep_kernel, n, LP, cp),
        out_shape=(
            jax.ShapeDtypeStruct((LP, 2 * K), BF16),
            jax.ShapeDtypeStruct((cp, K), F32),
            jax.ShapeDtypeStruct((1, W), F32),
            jax.ShapeDtypeStruct(sid.shape, jnp.int32),
        ),
        in_specs=[VMEM] * 5,
        out_specs=(VMEM,) * 4,
        scratch_shapes=[
            pltpu.VMEM((LP, 2 * K), BF16),
            pltpu.VMEM((n, pad, K), BF16),
            pltpu.VMEM((n, 1, pad), F32),
            pltpu.VMEM((n, room, K), BF16),
            pltpu.VMEM((1, W), F32),
            pltpu.VMEM((n, pad, K), BF16),
            pltpu.VMEM((n, 1, pad), F32),
            pltpu.VMEM((n, room, K), BF16),
            pltpu.VMEM((n, 1, W), F32),
        ] + [dma((n,))] * 12,
        compiler_params=pltpu.CompilerParams(collective_id=1, has_side_effects=True),
    )(sid, fm, chars, mean, cols)


def main_kernel(
    n, count_products, count_consumers, IC, JT, GR,
    C, tastes, coef, colpart, colmean, inv, ids, cols, sid, asked,
    out, sm,
    SV, HV, T, SCB, SH, DG, E, MS, CC, FL, WT, PO, PX, PR, YS, YR, ST,
    ms_s, ms_r, cc_s, cc_r, px_s, px_r, y_s, y_r, st_s, st_r, o_s, o_r, h_s, h_r,
):
    me = lax.axis_index("prod")
    cons = lax.axis_index("cons")
    core = lax.rem(cons, 2)
    partner = cons + 1 - 2 * core
    across = lax.rem(cons + 2, 4)
    LP = C.shape[0]
    LI, K = tastes.shape
    nc, nt = LI // IC, LP // JT
    half = out.shape[1] // 2
    block = inv.shape[1]

    barrier = pltpu.get_barrier_semaphore()
    for d in range(1, n):
        pl.semaphore_signal(barrier, inc=1, device_id={"prod": lax.rem(me + d, n)}, device_id_type=MESH)
    for d in range(1, 4):
        pl.semaphore_signal(barrier, inc=1, device_id={"cons": lax.rem(cons + d, 4)}, device_id_type=MESH)
    pl.semaphore_wait(barrier, n + 2)

    def cc_copy(d):
        return pltpu.make_async_remote_copy(
            colpart, CC.at[me], cc_s.at[d], cc_r.at[d],
            device_id={"prod": lax.rem(me + d, n)}, device_id_type=MESH,
        )

    def ms_copy(d, ic):
        return pltpu.make_async_remote_copy(
            MS.at[0, ic], MS.at[d, ic], ms_s.at[d, ic], ms_r.at[d, ic],
            device_id={"prod": lax.rem(me + d, n)}, device_id_type=MESH,
        )

    def each_peer(fn):
        def step(d, carry):
            fn(d)
            return carry
        lax.fori_loop(1, n, step, 0)

    each_peer(lambda d: cc_copy(d).start())
    T[:, :K] = tastes[...]
    lane = lax.broadcasted_iota(jnp.int32, (LI, C.shape[1] - K), 1)
    T[:, K:] = jnp.where(lane < 3, 1.0, 0.0).astype(BF16)
    CC[me] = colpart[...]

    def pass_one(ic, carry):
        i0 = pl.multiple_of(ic * IC, IC)
        tb = T[pl.ds(i0, IC), :]

        def utility(jt, m8):
            rows = pl.ds(pl.multiple_of(jt * JT, JT), JT)
            u = lax.dot_general(C[rows, :], tb, NT, preferred_element_type=F32)
            E[rows, pl.ds(i0, IC)] = u
            return jnp.maximum(m8, jnp.max(u.reshape(JT // 8, 8, IC), axis=0))

        m8 = lax.fori_loop(0, nt, utility, jnp.zeros((8, IC), F32))
        m = jnp.max(m8, axis=0, keepdims=True)

        def expo(jt, s8):
            rows = pl.ds(pl.multiple_of(jt * JT, JT), JT)
            e = jnp.exp(E[rows, pl.ds(i0, IC)] - m)
            E[rows, pl.ds(i0, IC)] = e
            return s8 + jnp.sum(e.reshape(JT // 8, 8, IC), axis=0)

        s8 = lax.fori_loop(0, nt, expo, jnp.zeros((8, IC), F32))
        MS[0, ic, 0:1, :] = m
        MS[0, ic, 1:2, :] = jnp.sum(s8, axis=0, keepdims=True)
        each_peer(lambda d: ms_copy(d, ic).start())
        return carry

    lax.fori_loop(0, nc, pass_one, 0)
    each_peer(lambda d: cc_copy(d).wait())
    ccv = CC[...].reshape(CC.shape[0] * CC.shape[1], CC.shape[2]).astype(BF16)
    cm = jnp.concatenate([turned(colmean[:, g * 128:(g + 1) * 128])[:, :1] for g in range(colmean.shape[1] // 128)], axis=0)

    def weights(ic, carry):
        each_peer(lambda d: ms_copy(d, ic).wait())
        i0 = pl.multiple_of(ic * IC, IC)
        peak = MS[0, ic, 0:1, :]
        for d in range(1, n):
            peak = jnp.maximum(peak, MS[d, ic, 0:1, :])
        den = jnp.exp(-peak)
        for d in range(n):
            den = den + MS[d, ic, 1:2, :] * jnp.exp(MS[d, ic, 0:1, :] - peak)
        f = count_products / den
        FL[:, pl.ds(i0, IC)] = jnp.exp(MS[0, ic, 0:1, :] - peak) * f
        cu = lax.dot_general(ccv, tastes[pl.ds(i0, IC), :], NT, preferred_element_type=F32) + cm
        w = coef[:, pl.ds(i0, IC)] * (f * jnp.exp(cu - peak))
        WT[pl.ds(i0, IC), :] = w.T.astype(BF16)
        return carry

    lax.fori_loop(0, nc, weights, 0)

    def px_copy(jt):
        rows = pl.ds(pl.multiple_of(jt * JT, JT), JT)
        return pltpu.make_async_remote_copy(
            PX.at[rows], PR.at[rows], px_s.at[jt], px_r.at[jt],
            device_id={"cons": partner}, device_id_type=MESH,
        )

    def y_copy(jt):
        rows = pl.ds(pl.multiple_of(jt * JT, JT), JT)
        return pltpu.make_async_remote_copy(
            YS.at[rows], YR.at[rows], y_s.at[jt], y_r.at[jt],
            device_id={"cons": across}, device_id_type=MESH,
        )

    def o_copy(jt):
        rows = pl.ds(pl.multiple_of(jt * JT, JT), JT)
        mine = pl.ds(pl.multiple_of(core * half, half), half)
        return pltpu.make_async_remote_copy(
            out.at[rows, mine], out.at[rows, mine], o_s.at[jt], o_r.at[jt],
            device_id={"cons": partner}, device_id_type=MESH,
        )

    def st_copy(d):
        return pltpu.make_async_remote_copy(
            ST.at[cons], ST.at[cons], st_s.at[d], st_r.at[d],
            device_id={"cons": lax.rem(cons + d, 4)}, device_id_type=MESH,
        )

    def forward(jt):
        rows = pl.ds(pl.multiple_of(jt * JT, JT), JT)
        px_copy(jt).wait()
        YS[rows, :] = (PO[rows, :] + PR[rows, :]).astype(BF16)
        y_copy(jt).start()

    def panel(jt, carry):
        rows = pl.ds(pl.multiple_of(jt * JT, JT), JT)

        def group(g, carry):
            g0 = pl.multiple_of(g * GR, GR)
            band = pl.ds(pl.multiple_of(jt * JT + g * GR, GR), GR)
            sh = jnp.zeros((GR, 128), F32)
            dg = jnp.zeros((GR, 128), F32)
            for b in range(LI // 128):
                at = pl.ds(b * 128, 128)
                sc = E[band, at] * FL[:, at]
                SCB[pl.ds(g0, GR), at] = sc.astype(BF16)
                sh = sh + sc
                dg = dg + sc * coef[:, at]
            SH[pl.ds(g0, GR), :] = sh
            DG[pl.ds(g0, GR), :] = dg
            return carry

        lax.fori_loop(0, JT // GR, group, 0)
        acc = jnp.dot(SCB[...], WT[...], preferred_element_type=F32)
        first, second = acc[:, :half], acc[:, half:]
        PO[rows, :] = jnp.where(core == 0, first, second)
        PX[rows, :] = jnp.where(core == 0, second, first)
        px_copy(jt).start()
        ST[cons, 0:1, rows] = jnp.sum(SH[...].T, axis=0, keepdims=True)
        ST[cons, 1:2, rows] = jnp.sum(DG[...].T, axis=0, keepdims=True)

        @pl.when(jt > 0)
        def _():
            forward(jt - 1)

        return carry

    lax.fori_loop(0, nt, panel, 0)
    for d in range(1, 4):
        st_copy(d).start()
    forward(nt - 1)
    for d in range(1, 4):
        st_copy(d).wait()
    sm[0:1, :] = (ST[0, 0:1, :] + ST[1, 0:1, :] + ST[2, 0:1, :] + ST[3, 0:1, :]) / count_consumers
    ST[0, 1:2, :] = (ST[0, 1:2, :] + ST[1, 1:2, :] + ST[2, 1:2, :] + ST[3, 1:2, :]) / count_consumers
    pad = sid.shape[2]
    spans = [(p, b) for p in range(n) for b in range(pad // 128)]

    def sorted_step(g, carry):
        rows = pl.ds(pl.multiple_of(g * 128, 128), 128)
        want = turned(ids[:, rows].astype(F32))
        share = turned(sm[0:1, rows])
        for p, b in spans:
            at = pl.ds(b * 128, 128)
            hit = jnp.where(want == sid[p, :, at].astype(F32), share, 0.0)
            SV[p, :, at] += jnp.sum(hit, axis=0, keepdims=True)
        return carry

    SV[...] = jnp.zeros_like(SV)
    lax.fori_loop(0, LP // 128, sorted_step, 0)

    def h_copy(d):
        peer = lax.rem(me + d, n)
        return pltpu.make_async_remote_copy(
            SV.at[peer], HV.at[me], h_s.at[d], h_r.at[d],
            device_id={"prod": peer}, device_id_type=MESH,
        )

    each_peer(lambda d: h_copy(d).start())
    HV[me] = SV[me]
    mine = pl.ds(pl.multiple_of(core * half, half), half)
    heads = cols[:, mine].astype(F32)

    def finish(jt, carry):
        y_copy(jt).wait()
        for b in range(JT // block):
            r0 = pl.multiple_of(jt * JT + b * block, block)
            rows = pl.ds(r0, block)
            fb = jt * (JT // block) + b
            x = (YS[rows, :].astype(F32) + YR[rows, :].astype(F32)) / count_consumers
            diag = jnp.broadcast_to(ST[0, 1:2, rows], (half, block)).T
            mine_ids = jnp.broadcast_to(ids[:, rows].astype(F32), (half, block)).T
            jac = x - jnp.where(mine_ids == heads, diag, 0.0)
            m = inv[fb]
            out[rows, mine] = jnp.dot(m, jac, precision=lax.Precision.HIGHEST, preferred_element_type=F32)
            share8 = jnp.broadcast_to(sm[0:1, rows], (8, block))
            mk = lax.dot_general(share8, m, NT, precision=lax.Precision.HIGHEST, preferred_element_type=F32)
            sm[1:2, rows] = mk[0:1, :]
        o_copy(jt).start()
        return carry

    lax.fori_loop(0, nt, finish, 0)

    each_peer(lambda d: h_copy(d).wait())
    sm[2:3, :] = jnp.zeros((1, LP), F32)

    def home_step(p, carry):
        for b in range(pad // 128):
            at = pl.ds(b * 128, 128)
            want = turned((asked[p, :, at] - me * LP).astype(F32))
            share = turned(HV[p, :, at])
            spot = lax.broadcasted_iota(jnp.int32, (128, 128), 1).astype(F32)
            for g in range(LP // 128):
                to = pl.ds(g * 128, 128)
                hit = jnp.where(want == spot + float(g * 128), share, 0.0)
                sm[2:3, to] += jnp.sum(hit, axis=0, keepdims=True)
        return carry

    lax.fori_loop(0, n, home_step, 0)

    def drain(jt, carry):
        o_copy(jt).wait()
        return carry

    lax.fori_loop(0, nt, drain, 0)


def run_main(n, caug, tastes, coef, colpart, colmean, inverses, ids, cols, sid, asked, count_products, count_consumers):
    LP, LI, W = caug.shape[0], tastes.shape[0], cols.shape[1]
    KA = caug.shape[1]
    IC, JT = min(512, LI), min(512, LP)
    nc, nt = LI // IC, LP // JT
    half = W // 2
    dma = pltpu.SemaphoreType.DMA
    return pl.pallas_call(
        functools.partial(main_kernel, n, float(count_products), float(count_consumers), IC, JT, min(32, JT)),
        out_shape=(jax.ShapeDtypeStruct((LP, W), F32), jax.ShapeDtypeStruct((3, LP), F32)),
        in_specs=[VMEM] * 10,
        out_specs=(VMEM, VMEM),
        scratch_shapes=[
            pltpu.VMEM(sid.shape, F32),
            pltpu.VMEM(sid.shape, F32),
            pltpu.VMEM((LI, KA), BF16),
            pltpu.VMEM((JT, LI), BF16),
            pltpu.VMEM((JT, 128), F32),
            pltpu.VMEM((JT, 128), F32),
            pltpu.VMEM((LP, LI), F32),
            pltpu.VMEM((n, nc, 2, IC), F32),
            pltpu.VMEM((n, W // n, KA // 2), F32),
            pltpu.VMEM((1, LI), F32),
            pltpu.VMEM((LI, W), BF16),
            pltpu.VMEM((LP, half), F32),
            pltpu.VMEM((LP, half), F32),
            pltpu.VMEM((LP, half), F32),
            pltpu.VMEM((LP, half), BF16),
            pltpu.VMEM((LP, half), BF16),
            pltpu.VMEM((4, 2, LP), F32),
            dma((n, nc)), dma((n, nc)), dma((n,)), dma((n,)),
            dma((nt,)), dma((nt,)), dma((nt,)), dma((nt,)),
            dma((4,)), dma((4,)), dma((nt,)), dma((nt,)), dma((n,)), dma((n,)),
        ],
        compiler_params=pltpu.CompilerParams(
            collective_id=7, has_side_effects=True, vmem_limit_bytes=LIMIT
        ),
    )(caug, tastes, coef, colpart, colmean, inverses, ids, cols, sid, asked)


def lanes(count):
    return -(-count // 128) * 128


def body(tastes, price_coef, characteristics, mean_utility, panel_cols, firm_map, inverses):
    n = lax.axis_size("prod")
    LP, K = characteristics.shape
    LI = tastes.shape[0]
    W = panel_cols.shape[0]
    count_products = LP * n
    count_consumers = LI * lax.axis_size("cons")
    pp = LP // n
    sid = jnp.pad(
        lax.sort(firm_map).reshape(n, 1, pp), ((0, 0), (0, 0), (0, lanes(pp) - pp)), constant_values=-1
    )
    cfirm, colpart, colmean, asked = prepare(
        n, sid, firm_map[None, :], characteristics, mean_utility[None, :], panel_cols[None, :]
    )
    response, sm = run_main(
        n, cfirm, tastes, price_coef[None, :], colpart, colmean, inverses,
        firm_map[None, :], panel_cols[None, :], sid, asked,
        count_products, count_consumers,
    )
    return sm[2], sm[1], response


def solution(mesh):
    return jax.shard_map(
        body,
        mesh=mesh,
        in_specs=(
            P("cons", None),
            P("cons"),
            P("prod", None),
            P("prod"),
            P(),
            P("prod"),
            P("prod", None, None),
        ),
        out_specs=(P("prod"), P("prod"), P("prod", None)),
        check_vma=False,
    )
```

profile of v0, /device:TPU:0, one launch (start us, length us, event | category | flops | bytes accessed | tf_op | source)
XLA Modules:
  0.0 93.7 jit_solution(9869305488518316967)
XLA Ops:
  0.6 5.7 %sort.14 = (s32[2048]{0:T(1024)}, s32[2048]{0:T(1024)}) sort(s32[2048]{0:T(1024)} %param.12, s32[2048]{0:T(1024)S(1)} %iota.3), dimensions={0}, to_apply=%region_0.0 | sort | flops 22528 | bytes 32768 | tf_op jit(solution)/shard_map/sort | solution.py:514
  6.4 26.0 %shard_map.94 = (bf16[2048,256]{1,0:T(8,128)(2,1)}, f32[32,128]{1,0:T(8,128)}, f32[1,256]{1,0:T(1,128)}, s32[8,1,256]{2,1,0:T(1,128)}) custom-call(s32[8,1,256]{2,1,0:T(1,128)} %bitcast.9, s32[1,2048]{1,0:T(1,128)} %bitcast.7, bf16[2048,128]{1,0:T(8,128)(2,1)} %chars.1, f32[1,2048]{1,0:T(1,128)} %bitcast.12, s32[1,256]{1,0:T(1,128)} %bitcast.15), custom_call_target="tpu_custom_call" | custom-call | tf_op jit(solution)/shard_map/pallas_call | solution.py:192
  32.4 56.8 %shard_map.95 = (f32[2048,256]{1,0:T(8,128)}, f32[3,2048]{1,0:T(4,128)}) custom-call(bf16[2048,256]{1,0:T(8,128)(2,1)} %get-tuple-element.12.C, bf16[4096,128]{1,0:T(8,128)(2,1)} %tastes.1, f32[1,4096]{1,0:T(1,128)} %bitcast.11, f32[32,128]{1,0:T(8,128)} %get-tuple-element.13.colpart, f32[1,256]{1,0:T(1,128)} %get-tuple-element.14.colmean, ...), custom_call_target="tpu_custom_call" | custom-call | tf_op jit(solution)/shard_map/pallas_call | solution.py:468
  89.2 1.5 %fusion = (f32[1,2048]{1,0:T(1,128)}, f32[1,2048]{1,0:T(1,128)}) fusion(f32[3,2048]{1,0:T(4,128)} %get-tuple-element.16), kind=kLoop, calls=%fused_computation | loop fusion | bytes 32768 | tf_op jit(solution)/shard_map/slice | solution.py:524
  90.6 3.0 %copy.11 = f32[2048,256]{1,0:T(8,128)} copy(f32[2048,256]{1,0:T(8,128)} %get-tuple-element.25) | data formatting | bytes 4194304
  (1 shorter events, 0.0 us)
where the time goes:
time: 94 us; the launch traced here: 93.7 us
  Pallas kernels  82.8 us (88%)
  other arithmetic  5.74 us (6%)
  local copies, waits for them, and re-layouts  4.5 us (5%)
    pallas_call x1, Pallas kernels, run_main(): pl.pallas_call(functools.partial(main_kernel, n, float(count_products), f...  56.8 us
    pallas_call x1, Pallas kernels, prepare(): pl.pallas_call(functools.partial(prep_kernel, n, LP, cp), out_shape=(jax....  26 us
    sort x1, other arithmetic, body(): lax.sort(firm_map).reshape(n, 1, pp)  5.74 us
    unnamed x1, local copies, waits for them, and re-layouts  3.04 us

commit v1 on v0

v1 whole, which is shorter than its diff:
```python
import functools
import jax
import jax.numpy as jnp
from jax import lax
from jax.experimental import pallas as pl
from jax.experimental.pallas import tpu as pltpu
from jax.sharding import PartitionSpec as P

F32 = jnp.float32
BF16 = jnp.bfloat16
NT = (((1,), (1,)), ((), ()))
MESH = pl.DeviceIdType.MESH
VMEM = pl.BlockSpec(memory_space=pltpu.VMEM)
LIMIT = 63 * 1024 * 1024


def lanes(count):
    return -(-count // 128) * 128


def turned(row):
    return jnp.broadcast_to(row, (128, 128)).T


def thirds(x):
    a = x.astype(BF16).astype(F32)
    b = (x - a).astype(BF16).astype(F32)
    return a, b, x - a - b


def split(column, width):
    lane = lax.broadcasted_iota(jnp.int32, (column.shape[0], width), 1)
    a, b, c = thirds(column)
    return jnp.where(lane == 0, a, jnp.where(lane == 1, b, jnp.where(lane == 2, c, 0.0))).astype(BF16)


def rows_of(shape):
    return lax.broadcasted_iota(jnp.int32, shape, 0).astype(F32)


def step_kernel(
    n, cp, room, pad, count_products, count_consumers, IC, WC, JT, GR,
    fm, cols, chars, mean, tastes, coef, inv,
    out, mk, home,
    CA, TA, CF, TB, MS2, KEY, BT, sid, asked,
    X, XM, R, RM, XC, XCM, RC, RCM, CP, CC,
    UA, MS, PK, FV, WT,
    UB, SCB, SH, DG, PO, PX, PR, YS, YR, ST, SV, HV,
    a_s, a_r, x_s, x_r, f_s, f_r, m_s, m_r, c_s, c_r, k_s, k_r, cc_s, cc_r,
    ms_s, ms_r, px_s, px_r, y_s, y_r, o_s, o_r, st_s, st_r, h_s, h_r,
):
    me = lax.axis_index("prod")
    cons = lax.axis_index("cons")
    core = lax.rem(cons, 2)
    partner = cons + 1 - 2 * core
    across = lax.rem(cons + 2, 4)
    LP, K = chars.shape
    LI = tastes.shape[0]
    W = cols.shape[1]
    half = W // 2
    block = inv.shape[1]
    pp = LP // n
    nb, pb = LP // 128, pad // 128
    nc, nw, nt = LI // IC, LI // WC, LP // JT
    base = me * LP

    barrier = pltpu.get_barrier_semaphore()
    for d in range(1, n):
        pl.semaphore_signal(barrier, inc=1, device_id={"prod": lax.rem(me + d, n)}, device_id_type=MESH)
    for d in range(1, 4):
        pl.semaphore_signal(barrier, inc=1, device_id={"cons": lax.rem(cons + d, 4)}, device_id_type=MESH)

    def loop(fn, lo=1):
        def step(d, carry):
            fn(d)
            return carry
        lax.fori_loop(lo, n, step, 0)

    def to_prod(src, dst, s, r, d):
        return pltpu.make_async_remote_copy(
            src, dst, s.at[d], r.at[d],
            device_id={"prod": lax.rem(me + d, n)}, device_id_type=MESH,
        )

    def to_cons(src, dst, s, r, peer):
        return pltpu.make_async_remote_copy(src, dst, s, r, device_id={"cons": peer}, device_id_type=MESH)

    fmf = fm[...].astype(F32)
    source = jnp.floor((fmf + 0.5) * (1.0 / LP))
    local = fmf - source * float(LP)
    owners = rows_of((n, 128))
    marks = jnp.concatenate(
        [jnp.where(source[:, b * 128:(b + 1) * 128] == owners, 1.0, 0.0) for b in range(nb)], axis=0
    )
    at0 = lax.broadcasted_iota(jnp.int32, (128, 128), 0)
    at1 = lax.broadcasted_iota(jnp.int32, (128, 128), 1)
    before = jnp.where(at0 < at1, 1.0, 0.0).astype(BF16)
    inner = jnp.dot(marks.astype(BF16), before, preferred_element_type=F32)
    totals = jnp.dot(marks.astype(BF16), jnp.ones((128, 128), BF16), preferred_element_type=F32)
    q0 = lax.broadcasted_iota(jnp.int32, (nb * n, nb * n), 0).astype(F32)
    q1 = lax.broadcasted_iota(jnp.int32, (nb * n, nb * n), 1).astype(F32)
    b0, b1 = jnp.floor((q0 + 0.5) * (1.0 / n)), jnp.floor((q1 + 0.5) * (1.0 / n))
    earlier = jnp.where((q0 - b0 * n == q1 - b1 * n) & (b1 < b0), 1.0, 0.0).astype(BF16)
    offset = jnp.dot(earlier, totals.astype(BF16), preferred_element_type=F32)
    placed = marks * (inner + offset)
    slot = jnp.concatenate(
        [jnp.sum(placed[b * n:(b + 1) * n], axis=0, keepdims=True) for b in range(nb)], axis=1
    )
    high = jnp.floor((slot + 0.5) * (1.0 / 128))
    KEY[...] = source * float(pb) + high
    BT[...] = jnp.where(slot - high * 128.0 == rows_of((128, LP)), 1.0, 0.0).astype(BF16)

    def scatter(parts):
        mask = KEY[...] == rows_of((n * pb, LP))
        left = jnp.concatenate([jnp.where(mask, p, 0.0) for p in parts], axis=0).astype(BF16)
        got = lax.dot_general(left, BT[...], NT, preferred_element_type=F32)
        return [got[k * n * pb:(k + 1) * n * pb] for k in range(len(parts))]

    upper = jnp.floor((local + 0.5) * (1.0 / 128))
    hi, lo = scatter([upper, local - upper * 128.0])
    q = rows_of((n * pb, 128))
    owner = jnp.floor((q + 0.5) * (1.0 / pb))
    place = (q - owner * pb) * 128.0 + lax.broadcasted_iota(jnp.int32, (n * pb, 128), 1).astype(F32)
    wanted = jnp.where(place < float(pp), owner * float(LP) + hi * 128.0 + lo, -1.0).astype(jnp.int32)
    for p in range(n):
        for b in range(pb):
            sid[p, :, b * 128:(b + 1) * 128] = wanted[p * pb + b:p * pb + b + 1]

    CA[:, :K] = chars[...]

    def widen(g, carry):
        rows = pl.ds(pl.multiple_of(g * 128, 128), 128)
        CA[rows, K:] = split(turned(mean[:, rows]), K)
        return carry

    lax.fori_loop(0, nb, widen, 0)
    TA[:, :K] = tastes[...]
    TA[:, K:] = jnp.where(lax.broadcasted_iota(jnp.int32, (LI, K), 1) < 3, 1.0, 0.0).astype(BF16)
    pl.semaphore_wait(barrier, n + 2)

    def a_copy(d):
        return to_prod(sid.at[lax.rem(me + d, n)], asked.at[me], a_s, a_r, d)

    loop(lambda d: a_copy(d).start())
    asked[me] = sid[me]

    def pick(wants):
        spot = lax.broadcasted_iota(jnp.int32, (128, 128), 1).astype(F32)
        bands = []
        for w in wants:
            want = turned((w - base).astype(F32))
            bands.append(jnp.concatenate(
                [jnp.where(want == spot + float(b * 128), 1.0, 0.0).astype(BF16) for b in range(nb)], axis=1
            ))
        got = jnp.dot(jnp.concatenate(bands, axis=0), CA[...], preferred_element_type=F32)
        means = []
        for k in range(len(wants)):
            t = got[k * 128:(k + 1) * 128, K:].T
            means.append(t[0:1] + (t[1:2] + t[2:3]))
        return got[:, :K].astype(BF16), means

    rows, means = pick([cols[:, g * 128:(g + 1) * 128] for g in range(W // 128)])
    XC[:, :cp, :] = rows.astype(F32).reshape(n, cp, K).astype(BF16)
    for g in range(W // 128):
        XCM[:, g * 128:(g + 1) * 128] = means[g]

    def c_copy(d):
        return to_prod(XC.at[lax.rem(me + d, n)], RC.at[me], c_s, c_r, d)

    def k_copy(d):
        return to_prod(XCM, RCM.at[me], k_s, k_r, d)

    loop(lambda d: c_copy(d).start())
    loop(lambda d: k_copy(d).start())
    RC[me] = XC[me]
    RCM[me] = XCM[...]

    def ms_copy(d, ic):
        return to_prod(MS.at[0, ic], MS.at[d, ic], ms_s.at[ic], ms_r.at[ic], d)

    def stats(ic, carry):
        i0 = pl.multiple_of(ic * IC, IC)
        u = lax.dot_general(CA[...], TA[pl.ds(i0, IC), :], NT, preferred_element_type=F32)
        UA[...] = u
        m = jnp.maximum(jnp.max(u, axis=0, keepdims=True), 0.0)
        s8 = jnp.sum(jnp.exp(UA[...] - m).reshape(LP // 8, 8, IC), axis=0)
        MS[0, ic, 0:1, :] = m
        MS[0, ic, 1:2, :] = jnp.sum(s8, axis=0, keepdims=True)
        loop(lambda d: ms_copy(d, ic).start())
        return carry

    def cc_copy(d):
        return to_prod(CP, CC.at[me], cc_s, cc_r, d)

    span = pad // 2
    part = pl.ds(pl.multiple_of(core * span, span), span)

    def x_copy(d):
        return to_prod(X.at[lax.rem(me + d, n), part], R.at[me, part], x_s, x_r, d)

    def m_copy(d):
        return to_prod(XM.at[lax.rem(me + d, n)], RM.at[me], m_s, m_r, d)

    def f_copy(d):
        src = lax.rem(me + n - d, n)
        return to_cons(R.at[src, part], R.at[src, part], f_s.at[d], f_r.at[d], partner)

    lax.fori_loop(0, nc // 2, stats, 0)
    loop(lambda d: c_copy(d).wait())
    loop(lambda d: k_copy(d).wait())
    total = RC[0, :cp, :].astype(F32)
    heads = RCM[0]
    for p in range(1, n):
        total = total + RC[p, :cp, :].astype(F32)
        heads = heads + RCM[p]
    CP[...] = total
    loop(lambda d: cc_copy(d).start())
    CC[me] = CP[...]

    def answer(d, carry):
        src = lax.rem(me + n - d, n)

        @pl.when(d > 0)
        def _():
            a_copy(lax.rem(n - d, n)).wait_send()
            a_copy(d).wait_recv()

        rows, means = pick([asked[src, :, b * 128:(b + 1) * 128] for b in range(pb)])
        X[src] = rows
        for b in range(pb):
            XM[src, :, b * 128:(b + 1) * 128] = means[b]

        @pl.when(d > 0)
        def _():
            back = lax.rem(n - d, n)
            x_copy(back).start()
            m_copy(back).start()

        return carry

    lax.fori_loop(0, n, answer, 0)
    R[me] = X[me]
    RM[me] = XM[me]
    lax.fori_loop(nc // 2, nc, stats, 0)

    def relay(d):
        x_copy(d).wait()
        f_copy(d).start()

    loop(relay)

    loop(lambda d: cc_copy(d).wait())
    ccv = CC[...].reshape(n * cp, K).astype(BF16)
    cm = jnp.concatenate([turned(heads[:, g * 128:(g + 1) * 128])[:, :1] for g in range(W // 128)], axis=0)

    def weights(ic):
        loop(lambda d: ms_copy(d, ic).wait())
        for w in range(IC // WC):
            i0 = pl.multiple_of(ic * IC + w * WC, WC)
            at = slice(w * WC, (w + 1) * WC)
            peak = MS[0, ic, 0:1, at]
            for d in range(1, n):
                peak = jnp.maximum(peak, MS[d, ic, 0:1, at])
            den = jnp.exp(-peak)
            for d in range(n):
                den = den + MS[d, ic, 1:2, at] * jnp.exp(MS[d, ic, 0:1, at] - peak)
            f = count_products / den
            PK[:, pl.ds(i0, WC)] = peak
            FV[:, pl.ds(i0, WC)] = f
            cu = lax.dot_general(ccv, tastes[pl.ds(i0, WC), :], NT, preferred_element_type=F32) + cm
            w = coef[:, pl.ds(i0, WC)] * (f * jnp.exp(cu - peak))
            WT[pl.ds(i0, WC), :] = w.T.astype(BF16)

    def weights_step(ic, carry):
        weights(ic)
        return carry

    lax.fori_loop(0, nc, weights_step, 0)

    loop(lambda d: m_copy(d).wait())
    loop(lambda d: f_copy(d).wait())

    def table(p, carry):
        at = pl.ds(pl.multiple_of(p * pad, pad), pad)
        TB[at, :K] = R[p]
        TB[at, K:] = jnp.concatenate(
            [split(turned(RM[p, :, b * 128:(b + 1) * 128]), K) for b in range(pb)], axis=0
        )
        return carry

    lax.fori_loop(0, n, table, 0)

    def firm(g, carry):
        bands = []
        for h in range(4):
            rows = pl.ds(pl.multiple_of(g * 512 + h * 128, 128), 128)
            want = turned(fm[:, rows].astype(F32))
            bands.append(jnp.concatenate(
                [
                    jnp.where(want == sid[p, :, b * 128:(b + 1) * 128].astype(F32), 1.0, 0.0).astype(BF16)
                    for p in range(n) for b in range(pb)
                ],
                axis=1,
            ))
        rows = pl.ds(pl.multiple_of(g * 512, 512), 512)
        CF[rows, :] = jnp.dot(jnp.concatenate(bands, axis=0), TB[...], preferred_element_type=F32).astype(BF16)
        return carry

    lax.fori_loop(0, LP // 512, firm, 0)

    def halves(fb, carry):
        m = inv[fb]
        h = m.astype(BF16)
        MS2[fb, :, :block] = h
        MS2[fb, :, block:] = (m - h.astype(F32)).astype(BF16)
        return carry

    lax.fori_loop(0, LP // block, halves, 0)

    def tile_rows(jt):
        return pl.ds(pl.multiple_of(jt * JT, JT), JT)

    def px_copy(jt):
        rows = tile_rows(jt)
        return to_cons(PX.at[rows], PR.at[rows], px_s.at[jt], px_r.at[jt], partner)

    def y_copy(jt):
        rows = tile_rows(jt)
        return to_cons(YS.at[rows], YR.at[rows], y_s.at[jt], y_r.at[jt], across)

    mine = pl.ds(pl.multiple_of(core * half, half), half)

    def o_copy(jt):
        rows = tile_rows(jt)
        return to_cons(out.at[rows, mine], out.at[rows, mine], o_s.at[jt], o_r.at[jt], partner)

    def st_copy(d):
        return to_cons(ST.at[cons], ST.at[cons], st_s.at[d], st_r.at[d], lax.rem(cons + d, 4))

    def forward(jt):
        rows = tile_rows(jt)
        px_copy(jt).wait()
        YS[rows, :] = (PO[rows, :] + PR[rows, :]).astype(BF16)
        y_copy(jt).start()

    def finish(jt):
        y_copy(jt).wait()
        for b in range(JT // block):
            rows = pl.ds(pl.multiple_of(jt * JT + b * block, block), block)
            x = (YS[rows, :].astype(F32) + YR[rows, :].astype(F32)) / count_consumers
            h = x.astype(BF16)
            pair = jnp.concatenate([h, (x - h.astype(F32)).astype(BF16)], axis=1)
            both = jnp.concatenate([pair, pair], axis=0)
            r = jnp.dot(MS2[jt * (JT // block) + b], both, preferred_element_type=F32)
            out[rows, mine] = r[:, :half] + r[:, half:]
        o_copy(jt).start()

    heads_row = cols[...].astype(F32)

    def panel(jt, carry):
        rows = tile_rows(jt)
        UB[...] = lax.dot_general(CF[rows, :], TA[...], NT, preferred_element_type=F32)
        for g in range(JT // GR):
            band = pl.ds(g * GR, GR)
            sh = jnp.zeros((GR, 128), F32)
            dg = jnp.zeros((GR, 128), F32)
            for b in range(LI // 128):
                at = pl.ds(b * 128, 128)
                sc = jnp.exp(UB[band, at] - PK[:, at]) * FV[:, at]
                SCB[band, at] = sc.astype(BF16)
                sh = sh + sc
                dg = dg + sc * coef[:, at]
            SH[band, :] = sh
            DG[band, :] = dg
        acc = jnp.dot(SCB[...], WT[...], preferred_element_type=F32)
        ST[cons, 0:1, rows] = jnp.sum(SH[...].T, axis=0, keepdims=True)
        diag = jnp.sum(DG[...], axis=1, keepdims=True)
        ids = jnp.concatenate(
            [
                turned(fm[:, pl.ds(pl.multiple_of(jt * JT + b * 128, 128), 128)].astype(F32))[:, :1]
                for b in range(JT // 128)
            ],
            axis=0,
        )
        acc = acc - jnp.where(ids == heads_row, diag, 0.0)
        first, second = acc[:, :half], acc[:, half:]
        PO[rows, :] = jnp.where(core == 0, first, second)
        PX[rows, :] = jnp.where(core == 0, second, first)
        px_copy(jt).start()

        @pl.when(jt > 0)
        def _():
            forward(jt - 1)

        @pl.when(jt > 1)
        def _():
            finish(jt - 2)

        return carry

    lax.fori_loop(0, nt, panel, 0)
    for d in range(1, 4):
        st_copy(d).start()
    forward(nt - 1)
    for d in range(1, 4):
        st_copy(d).wait()
    share = (ST[0] + ST[1] + ST[2] + ST[3]) / count_consumers
    sums = scatter(thirds(share))
    slots = sums[0] + (sums[1] + sums[2])
    for p in range(n):
        for b in range(pb):
            SV[p, :, b * 128:(b + 1) * 128] = slots[p * pb + b:p * pb + b + 1]

    def h_copy(d):
        return to_prod(SV.at[lax.rem(me + d, n)], HV.at[me], h_s, h_r, d)

    loop(lambda d: h_copy(d).start())
    HV[me] = SV[me]
    for t in range(max(nt - 2, 0), nt - 1):
        finish(t)
    s1 = share.astype(BF16)
    s2 = (share - s1.astype(F32)).astype(BF16)
    for fb in range(LP // block):
        at = slice(fb * block, (fb + 1) * block)
        pair = jnp.concatenate([s1[:, at], s1[:, at]], axis=1).astype(F32)
        rest = jnp.concatenate([s2[:, at], s2[:, at]], axis=1).astype(F32)
        left = jnp.concatenate([jnp.broadcast_to(pair, (8, 2 * block)), jnp.broadcast_to(rest, (8, 2 * block))], axis=0)
        r = lax.dot_general(left.astype(BF16), MS2[fb], NT, preferred_element_type=F32)
        mk[fb:fb + 1, :] = r[0:1] + r[8:9]
    finish(nt - 1)

    loop(lambda d: h_copy(d).wait())
    ids = jnp.concatenate([asked[p] for p in range(n)], axis=1) - base
    idf = ids.astype(F32)
    up = jnp.floor((idf + 0.5) * (1.0 / 128))
    right = jnp.where(idf - up * 128.0 == rows_of((128, n * pad)), 1.0, 0.0).astype(BF16)
    mask = up == rows_of((nb, n * pad))
    back = jnp.concatenate([HV[p] for p in range(n)], axis=1)
    left = jnp.concatenate([jnp.where(mask, p, 0.0) for p in thirds(back)], axis=0).astype(BF16)
    got = lax.dot_general(left, right, NT, preferred_element_type=F32)
    home[...] = got[:nb] + (got[nb:2 * nb] + got[2 * nb:])

    def drain(jt, carry):
        o_copy(jt).wait()
        return carry

    lax.fori_loop(0, nt, drain, 0)


def run(n, count_products, count_consumers, fm, cols, chars, mean, tastes, coef, inv):
    LP, K = chars.shape
    LI, W = tastes.shape[0], cols.shape[1]
    block = inv.shape[1]
    half = W // 2
    cp = W // n
    room = -(-cp // 16) * 16
    pad = lanes(LP // n)
    IC, WC, JT, GR = min(1024, LI), min(512, LI), min(512, LP), 32
    nc, nt = LI // IC, LP // JT
    nb, pb = LP // 128, pad // 128
    dma = pltpu.SemaphoreType.DMA
    vm = pltpu.VMEM
    I32 = jnp.int32
    return pl.pallas_call(
        functools.partial(
            step_kernel, n, cp, room, pad, float(count_products), float(count_consumers), IC, WC, JT, GR
        ),
        out_shape=(
            jax.ShapeDtypeStruct((LP, W), F32),
            jax.ShapeDtypeStruct((LP // block, block), F32),
            jax.ShapeDtypeStruct((nb, 128), F32),
        ),
        in_specs=[VMEM] * 7,
        out_specs=(VMEM,) * 3,
        scratch_shapes=[
            vm((LP, 2 * K), BF16), vm((LI, 2 * K), BF16), vm((LP, 2 * K), BF16), vm((n * pad, 2 * K), BF16),
            vm((LP // block, block, 2 * block), BF16), vm((1, LP), F32), vm((128, LP), BF16),
            vm((n, 1, pad), I32), vm((n, 1, pad), I32),
            vm((n, pad, K), BF16), vm((n, 1, pad), F32), vm((n, pad, K), BF16), vm((n, 1, pad), F32),
            vm((n, room, K), BF16), vm((1, W), F32), vm((n, room, K), BF16), vm((n, 1, W), F32),
            vm((cp, K), F32), vm((n, cp, K), F32),
            vm((LP, IC), F32), vm((n, nc, 2, IC), F32), vm((1, LI), F32), vm((1, LI), F32), vm((LI, W), BF16),
            vm((JT, LI), F32), vm((JT, LI), BF16), vm((JT, 128), F32), vm((JT, 128), F32),
            vm((LP, half), F32), vm((LP, half), F32), vm((LP, half), F32),
            vm((LP, half), BF16), vm((LP, half), BF16),
            vm((4, 1, LP), F32), vm((n, 1, pad), F32), vm((n, 1, pad), F32),
        ] + [dma((n,))] * 14 + [dma((nc, n))] * 2 + [dma((nt,))] * 6 + [dma((4,))] * 2 + [dma((n,))] * 2,
        compiler_params=pltpu.CompilerParams(collective_id=1, has_side_effects=True, vmem_limit_bytes=LIMIT),
    )(fm, cols, chars, mean, tastes, coef, inv)


def body(tastes, price_coef, characteristics, mean_utility, panel_cols, firm_map, inverses):
    n = lax.axis_size("prod")
    LP = characteristics.shape[0]
    response, markup, shares = run(
        n, LP * n, tastes.shape[0] * lax.axis_size("cons"),
        firm_map[None, :], panel_cols[None, :], characteristics, mean_utility[None, :],
        tastes, price_coef[None, :], inverses,
    )
    return shares.reshape(LP), markup.reshape(LP), response


def solution(mesh):
    return jax.shard_map(
        body,
        mesh=mesh,
        in_specs=(
            P("cons", None),
            P("cons"),
            P("prod", None),
            P("prod"),
            P(),
            P("prod"),
            P("prod", None, None),
        ),
        out_specs=(P("prod"), P("prod"), P("prod", None)),
        check_vma=False,
    )
```

time: 94 us -> 68.3 us (0.73)
  Pallas kernels: 82.8 us -> 61.8 us
  other arithmetic: 5.74 us -> 0 us
  local copies, waits for them, and re-layouts: 4.5 us -> 5.63 us
    pallas_call x2 -> x1, Pallas kernels: 82.8 us -> 61.8 us  [run(): pl.pallas_call(functools.partial(step_kernel, n, cp, room, pad, float(cou...]
    sort x1 -> x0, other arithmetic: 5.74 us -> none  [body(): lax.sort(firm_map).reshape(n, 1, pp)]
    unnamed x1 -> x3, local copies, waits for them, and re-layouts: 3.04 us -> 5.63 us
    slice x1 -> x0, local copies, waits for them, and re-layouts: 1.45 us -> none  [body(): return (sm[2], sm[1], response)]
where the time goes in v1:
time: 68.3 us; the launch traced here: 68 us
  Pallas kernels  61.8 us (90%)
  local copies, waits for them, and re-layouts  5.63 us (8%)
    pallas_call x1, Pallas kernels, run(): pl.pallas_call(functools.partial(step_kernel, n, cp, room, pad, float(cou...  61.8 us
    unnamed x3, local copies, waits for them, and re-layouts  5.63 us

profile of v1, /device:TPU:0, one launch (start us, length us, event | category | flops | bytes accessed | tf_op | source)
XLA Modules:
  0.0 68.0 jit_solution(18202002816355613655)
XLA Ops:
  0.6 61.8 %shard_map.94 = (f32[2048,256]{1,0:T(8,128)}, f32[16,128]{1,0:T(8,128)}, f32[16,128]{1,0:T(8,128)}) custom-call(s32[1,2048]{1,0:T(1,128)} %bitcast.7, s32[1,256]{1,0:T(1,128)} %bitcast.11, bf16[2048,128]{1,0:T(8,128)(2,1)} %chars.1, f32[1,2048]{1,0:T(1,128)} %bitcast.8, bf16[4096,128]{1,0:T(8,128)(2,1)} %tastes.1, f32[1,4096]{1,0:T(1,128)} %bitcast.6, ...), custom_call_target="tpu_custom_call" | custom-call | tf_op jit(solution)/shard_map/pallas_call | solution.py:464
  62.4 1.3 %copy.13 = f32[2048]{0:T(1024)} copy(f32[2048]{0:T(1024)} %bitcast.10) | data formatting | bytes 16384
  63.7 1.3 %copy.14 = f32[2048]{0:T(1024)} copy(f32[2048]{0:T(1024)} %bitcast.9) | data formatting | bytes 16384
  65.0 3.0 %copy.15 = f32[2048,256]{1,0:T(8,128)} copy(f32[2048,256]{1,0:T(8,128)} %get-tuple-element.14) | data formatting | bytes 4194304

commit v2 on v1

--- a/solution.py
+++ b/solution.py
@@ -40,13 +40,13 @@
 
 def step_kernel(
     n, cp, room, pad, count_products, count_consumers, IC, WC, JT, GR,
-    fm, cols, chars, mean, tastes, coef, inv,
-    out, mk, home,
-    CA, TA, CF, TB, MS2, KEY, BT, sid, asked,
+    fm, cols, chars, mean, tastes, coef,
+    out, srow, home,
+    CA, TA, CF, TB, KEY, BT, sid, asked,
     X, XM, R, RM, XC, XCM, RC, RCM, CP, CC,
     UA, MS, PK, FV, WT,
-    UB, SCB, SH, DG, PO, PX, PR, YS, YR, ST, SV, HV,
-    a_s, a_r, x_s, x_r, f_s, f_r, m_s, m_r, c_s, c_r, k_s, k_r, cc_s, cc_r,
+    XO, UB, SCB, SH, DG, PO, PX, PR, YS, YR, ST, SV, HV,
+    i_s, w_s, a_s, a_r, x_s, x_r, f_s, f_r, m_s, m_r, c_s, c_r, k_s, k_r, cc_s, cc_r,
     ms_s, ms_r, px_s, px_r, y_s, y_r, o_s, o_r, st_s, st_r, h_s, h_r,
 ):
     me = lax.axis_index("prod")
@@ -58,7 +58,6 @@
     LI = tastes.shape[0]
     W = cols.shape[1]
     half = W // 2
-    block = inv.shape[1]
     pp = LP // n
     nb, pb = LP // 128, pad // 128
     nc, nw, nt = LI // IC, LI // WC, LP // JT
@@ -78,12 +77,22 @@
 
     def to_prod(src, dst, s, r, d):
         return pltpu.make_async_remote_copy(
-            src, dst, s.at[d], r.at[d],
+            src, dst, s, r,
             device_id={"prod": lax.rem(me + d, n)}, device_id_type=MESH,
         )
 
+    rest = pl.ds(0, n - 1)
+
+    def all_of(ref, s, r):
+        return to_prod(ref, ref, s, r, 1)
+
     def to_cons(src, dst, s, r, peer):
         return pltpu.make_async_remote_copy(src, dst, s, r, device_id={"cons": peer}, device_id_type=MESH)
+
+    load_chars = pltpu.make_async_copy(chars, CA.at[:, pl.ds(0, K)], i_s.at[0])
+    load_tastes = pltpu.make_async_copy(tastes, TA.at[:, pl.ds(0, K)], i_s.at[1])
+    load_chars.start()
+    load_tastes.start()
 
     fmf = fm[...].astype(F32)
     source = jnp.floor((fmf + 0.5) * (1.0 / LP))
@@ -126,23 +135,18 @@
         for b in range(pb):
             sid[p, :, b * 128:(b + 1) * 128] = wanted[p * pb + b:p * pb + b + 1]
 
-    CA[:, :K] = chars[...]
-
-    def widen(g, carry):
-        rows = pl.ds(pl.multiple_of(g * 128, 128), 128)
-        CA[rows, K:] = split(turned(mean[:, rows]), K)
-        return carry
-
-    lax.fori_loop(0, nb, widen, 0)
-    TA[:, :K] = tastes[...]
-    TA[:, K:] = jnp.where(lax.broadcasted_iota(jnp.int32, (LI, K), 1) < 3, 1.0, 0.0).astype(BF16)
     pl.semaphore_wait(barrier, n + 2)
 
     def a_copy(d):
-        return to_prod(sid.at[lax.rem(me + d, n)], asked.at[me], a_s, a_r, d)
+        return to_prod(sid.at[lax.rem(me + d, n)], asked.at[me], a_s.at[0], a_r.at[d], d)
 
     loop(lambda d: a_copy(d).start())
     asked[me] = sid[me]
+
+    for g in range(nb):
+        CA[g * 128:(g + 1) * 128, K:] = split(turned(mean[:, g * 128:(g + 1) * 128]), K)
+    TA[:, K:] = jnp.where(lax.broadcasted_iota(jnp.int32, (LI, K), 1) < 3, 1.0, 0.0).astype(BF16)
+    load_chars.wait()
 
     def pick(wants):
         spot = lax.broadcasted_iota(jnp.int32, (128, 128), 1).astype(F32)
@@ -165,10 +169,10 @@
         XCM[:, g * 128:(g + 1) * 128] = means[g]
 
     def c_copy(d):
-        return to_prod(XC.at[lax.rem(me + d, n)], RC.at[me], c_s, c_r, d)
+        return to_prod(XC.at[lax.rem(me + d, n)], RC.at[me], c_s.at[0], c_r.at[0], d)
 
     def k_copy(d):
-        return to_prod(XCM, RCM.at[me], k_s, k_r, d)
+        return to_prod(XCM, RCM.at[me], k_s.at[0], k_r.at[0], d)
 
     loop(lambda d: c_copy(d).start())
     loop(lambda d: k_copy(d).start())
@@ -190,24 +194,25 @@
         return carry
 
     def cc_copy(d):
-        return to_prod(CP, CC.at[me], cc_s, cc_r, d)
+        return to_prod(CP, CC.at[me], cc_s.at[0], cc_r.at[0], d)
 
     span = pad // 2
     part = pl.ds(pl.multiple_of(core * span, span), span)
 
     def x_copy(d):
-        return to_prod(X.at[lax.rem(me + d, n), part], R.at[me, part], x_s, x_r, d)
+        return to_prod(X.at[lax.rem(me + d, n), part], R.at[me, part], x_s.at[0], x_r.at[d], d)
 
     def m_copy(d):
-        return to_prod(XM.at[lax.rem(me + d, n)], RM.at[me], m_s, m_r, d)
+        return to_prod(XM.at[lax.rem(me + d, n)], RM.at[me], m_s.at[0], m_r.at[0], d)
 
     def f_copy(d):
         src = lax.rem(me + n - d, n)
-        return to_cons(R.at[src, part], R.at[src, part], f_s.at[d], f_r.at[d], partner)
-
-    lax.fori_loop(0, nc // 2, stats, 0)
-    loop(lambda d: c_copy(d).wait())
-    loop(lambda d: k_copy(d).wait())
+        return to_cons(R.at[src, part], R.at[src, part], f_s.at[0], f_r.at[0], partner)
+
+    load_tastes.wait()
+    lax.fori_loop(0, 1, stats, 0)
+    all_of(RC.at[rest], c_s.at[0], c_r.at[0]).wait()
+    all_of(RCM.at[rest], k_s.at[0], k_r.at[0]).wait()
     total = RC[0, :cp, :].astype(F32)
     heads = RCM[0]
     for p in range(1, n):
@@ -217,44 +222,75 @@
     loop(lambda d: cc_copy(d).start())
     CC[me] = CP[...]
 
-    def answer(d, carry):
-        src = lax.rem(me + n - d, n)
-
-        @pl.when(d > 0)
+    def answer(k, carry):
+        sources = [lax.rem(me + n - 2 * k - h, n) for h in range(2)]
+
+        @pl.when(k > 0)
         def _():
-            a_copy(lax.rem(n - d, n)).wait_send()
-            a_copy(d).wait_recv()
-
-        rows, means = pick([asked[src, :, b * 128:(b + 1) * 128] for b in range(pb)])
-        X[src] = rows
-        for b in range(pb):
-            XM[src, :, b * 128:(b + 1) * 128] = means[b]
-
-        @pl.when(d > 0)
+            a_copy(2 * k).wait_recv()
+
+        a_copy(2 * k + 1).wait_recv()
+        rows, means = pick([asked[src, :, b * 128:(b + 1) * 128] for src in sources for b in range(pb)])
+        for h, src in enumerate(sources):
+            X[src] = rows[h * pad:(h + 1) * pad]
+            for b in range(pb):
+                XM[src, :, b * 128:(b + 1) * 128] = means[h * pb + b]
+
+        @pl.when(k > 0)
         def _():
-            back = lax.rem(n - d, n)
-            x_copy(back).start()
-            m_copy(back).start()
-
+            x_copy(n - 2 * k).start()
+            m_copy(n - 2 * k).start()
+
+        x_copy(n - 2 * k - 1).start()
+        m_copy(n - 2 * k - 1).start()
         return carry
 
-    lax.fori_loop(0, n, answer, 0)
+    lax.fori_loop(0, n // 2, answer, 0)
+    all_of(sid.at[rest], a_s.at[0], a_r.at[0]).wait_send()
     R[me] = X[me]
     RM[me] = XM[me]
-    lax.fori_loop(nc // 2, nc, stats, 0)
+    lax.fori_loop(1, nc, stats, 0)
 
     def relay(d):
-        x_copy(d).wait()
+        x_copy(d).wait_recv()
         f_copy(d).start()
 
     loop(relay)
-
-    loop(lambda d: cc_copy(d).wait())
+    all_of(X.at[rest, part], x_s.at[0], x_r.at[0]).wait_send()
+
+    all_of(RM.at[rest], m_s.at[0], m_r.at[0]).wait()
+    all_of(R.at[rest, part], f_s.at[0], f_r.at[0]).wait()
+
+    for p in range(n):
+        TB[p * pad:(p + 1) * pad, :K] = R[p]
+        for b in range(pb):
+            at = p * pad + b * 128
+            TB[at:at + 128, K:] = split(turned(RM[p, :, b * 128:(b + 1) * 128]), K)
+
+    def firm(g, carry):
+        bands = []
+        for h in range(8):
+            rows = pl.ds(pl.multiple_of(g * 1024 + h * 128, 128), 128)
+            want = turned(fm[:, rows].astype(F32))
+            bands.append(jnp.concatenate(
+                [
+                    jnp.where(want == sid[p, :, b * 128:(b + 1) * 128].astype(F32), 1.0, 0.0).astype(BF16)
+                    for p in range(n) for b in range(pb)
+                ],
+                axis=1,
+            ))
+        rows = pl.ds(pl.multiple_of(g * 1024, 1024), 1024)
+        CF[rows, :] = jnp.dot(jnp.concatenate(bands, axis=0), TB[...], preferred_element_type=F32).astype(BF16)
+        return carry
+
+    lax.fori_loop(0, LP // 1024, firm, 0)
+
+    all_of(CC.at[rest], cc_s.at[0], cc_r.at[0]).wait()
     ccv = CC[...].reshape(n * cp, K).astype(BF16)
     cm = jnp.concatenate([turned(heads[:, g * 128:(g + 1) * 128])[:, :1] for g in range(W // 128)], axis=0)
 
     def weights(ic):
-        loop(lambda d: ms_copy(d, ic).wait())
+        all_of(MS.at[pl.ds(1, n - 1), ic], ms_s.at[ic], ms_r.at[ic]).wait()
         for w in range(IC // WC):
             i0 = pl.multiple_of(ic * IC + w * WC, WC)
             at = slice(w * WC, (w + 1) * WC)
@@ -267,9 +303,9 @@
             f = count_products / den
             PK[:, pl.ds(i0, WC)] = peak
             FV[:, pl.ds(i0, WC)] = f
-            cu = lax.dot_general(ccv, tastes[pl.ds(i0, WC), :], NT, preferred_element_type=F32) + cm
+            cu = lax.dot_general(ccv, TA[pl.ds(i0, WC), :K], NT, preferred_element_type=F32) + cm
             w = coef[:, pl.ds(i0, WC)] * (f * jnp.exp(cu - peak))
-            WT[pl.ds(i0, WC), :] = w.T.astype(BF16)
+            WT[pl.ds(i0, WC), :] = w.astype(BF16).T
 
     def weights_step(ic, carry):
         weights(ic)
@@ -277,83 +313,51 @@
 
     lax.fori_loop(0, nc, weights_step, 0)
 
-    loop(lambda d: m_copy(d).wait())
-    loop(lambda d: f_copy(d).wait())
-
-    def table(p, carry):
-        at = pl.ds(pl.multiple_of(p * pad, pad), pad)
-        TB[at, :K] = R[p]
-        TB[at, K:] = jnp.concatenate(
-            [split(turned(RM[p, :, b * 128:(b + 1) * 128]), K) for b in range(pb)], axis=0
-        )
-        return carry
-
-    lax.fori_loop(0, n, table, 0)
-
-    def firm(g, carry):
-        bands = []
-        for h in range(4):
-            rows = pl.ds(pl.multiple_of(g * 512 + h * 128, 128), 128)
-            want = turned(fm[:, rows].astype(F32))
-            bands.append(jnp.concatenate(
-                [
-                    jnp.where(want == sid[p, :, b * 128:(b + 1) * 128].astype(F32), 1.0, 0.0).astype(BF16)
-                    for p in range(n) for b in range(pb)
-                ],
-                axis=1,
-            ))
-        rows = pl.ds(pl.multiple_of(g * 512, 512), 512)
-        CF[rows, :] = jnp.dot(jnp.concatenate(bands, axis=0), TB[...], preferred_element_type=F32).astype(BF16)
-        return carry
-
-    lax.fori_loop(0, LP // 512, firm, 0)
-
-    def halves(fb, carry):
-        m = inv[fb]
-        h = m.astype(BF16)
-        MS2[fb, :, :block] = h
-        MS2[fb, :, block:] = (m - h.astype(F32)).astype(BF16)
-        return carry
-
-    lax.fori_loop(0, LP // block, halves, 0)
-
     def tile_rows(jt):
         return pl.ds(pl.multiple_of(jt * JT, JT), JT)
 
     def px_copy(jt):
         rows = tile_rows(jt)
-        return to_cons(PX.at[rows], PR.at[rows], px_s.at[jt], px_r.at[jt], partner)
+        return to_cons(PX.at[rows], PR.at[rows], px_s.at[0], px_r.at[jt], partner)
 
     def y_copy(jt):
         rows = tile_rows(jt)
-        return to_cons(YS.at[rows], YR.at[rows], y_s.at[jt], y_r.at[jt], across)
+        return to_cons(YS.at[rows], YR.at[rows], y_s.at[0], y_r.at[jt], across)
 
     mine = pl.ds(pl.multiple_of(core * half, half), half)
 
     def o_copy(jt):
         rows = tile_rows(jt)
-        return to_cons(out.at[rows, mine], out.at[rows, mine], o_s.at[jt], o_r.at[jt], partner)
-
-    def st_copy(d):
-        return to_cons(ST.at[cons], ST.at[cons], st_s.at[d], st_r.at[d], lax.rem(cons + d, 4))
+        return to_cons(XO.at[rows, mine], XO.at[rows, mine], o_s.at[0], o_r.at[jt], partner)
+
+    theirs = pl.ds(pl.multiple_of((1 - core) * half, half), half)
+
+    def write(jt, which):
+        rows = tile_rows(jt)
+        return pltpu.make_async_copy(XO.at[rows, which], out.at[rows, which], w_s.at[0])
+
+    def st_copy(d, jt):
+        rows = tile_rows(jt)
+        return to_cons(
+            ST.at[cons, :, rows], ST.at[cons, :, rows], st_s.at[0], st_r.at[0], lax.rem(cons + d, 4)
+        )
 
     def forward(jt):
         rows = tile_rows(jt)
-        px_copy(jt).wait()
+        px_copy(jt).wait_recv()
         YS[rows, :] = (PO[rows, :] + PR[rows, :]).astype(BF16)
         y_copy(jt).start()
 
     def finish(jt):
-        y_copy(jt).wait()
-        for b in range(JT // block):
-            rows = pl.ds(pl.multiple_of(jt * JT + b * block, block), block)
-            x = (YS[rows, :].astype(F32) + YR[rows, :].astype(F32)) / count_consumers
-            h = x.astype(BF16)
-            pair = jnp.concatenate([h, (x - h.astype(F32)).astype(BF16)], axis=1)
-            both = jnp.concatenate([pair, pair], axis=0)
-            r = jnp.dot(MS2[jt * (JT // block) + b], both, preferred_element_type=F32)
-            out[rows, mine] = r[:, :half] + r[:, half:]
+        y_copy(jt).wait_recv()
+        rows = tile_rows(jt)
+        XO[rows, mine] = (YS[rows, :].astype(F32) + YR[rows, :].astype(F32)) / count_consumers
         o_copy(jt).start()
+        write(jt, mine).start()
+
+    def gather(jt):
+        o_copy(jt).wait_recv()
+        write(jt, theirs).start()
 
     heads_row = cols[...].astype(F32)
 
@@ -374,6 +378,8 @@
             DG[band, :] = dg
         acc = jnp.dot(SCB[...], WT[...], preferred_element_type=F32)
         ST[cons, 0:1, rows] = jnp.sum(SH[...].T, axis=0, keepdims=True)
+        for d in range(1, 4):
+            st_copy(d, jt).start()
         diag = jnp.sum(DG[...], axis=1, keepdims=True)
         ids = jnp.concatenate(
             [
@@ -392,18 +398,20 @@
         def _():
             forward(jt - 1)
 
-        @pl.when(jt > 1)
+        @pl.when(jt > 3)
         def _():
-            finish(jt - 2)
+            finish(jt - 4)
+
+        @pl.when(jt > 4)
+        def _():
+            gather(jt - 5)
 
         return carry
 
     lax.fori_loop(0, nt, panel, 0)
-    for d in range(1, 4):
-        st_copy(d).start()
     forward(nt - 1)
-    for d in range(1, 4):
-        st_copy(d).wait()
+
+    all_of(ST.at[pl.ds(0, 3)], st_s.at[0], st_r.at[0]).wait()
     share = (ST[0] + ST[1] + ST[2] + ST[3]) / count_consumers
     sums = scatter(thirds(share))
     slots = sums[0] + (sums[1] + sums[2])
@@ -412,24 +420,16 @@
             SV[p, :, b * 128:(b + 1) * 128] = slots[p * pb + b:p * pb + b + 1]
 
     def h_copy(d):
-        return to_prod(SV.at[lax.rem(me + d, n)], HV.at[me], h_s, h_r, d)
+        return to_prod(SV.at[lax.rem(me + d, n)], HV.at[me], h_s.at[0], h_r.at[0], d)
 
     loop(lambda d: h_copy(d).start())
     HV[me] = SV[me]
-    for t in range(max(nt - 2, 0), nt - 1):
+    for t in range(max(nt - 4, 0), nt - 1):
         finish(t)
-    s1 = share.astype(BF16)
-    s2 = (share - s1.astype(F32)).astype(BF16)
-    for fb in range(LP // block):
-        at = slice(fb * block, (fb + 1) * block)
-        pair = jnp.concatenate([s1[:, at], s1[:, at]], axis=1).astype(F32)
-        rest = jnp.concatenate([s2[:, at], s2[:, at]], axis=1).astype(F32)
-        left = jnp.concatenate([jnp.broadcast_to(pair, (8, 2 * block)), jnp.broadcast_to(rest, (8, 2 * block))], axis=0)
-        r = lax.dot_general(left.astype(BF16), MS2[fb], NT, preferred_element_type=F32)
-        mk[fb:fb + 1, :] = r[0:1] + r[8:9]
+    srow[...] = share
     finish(nt - 1)
 
-    loop(lambda d: h_copy(d).wait())
+    all_of(HV.at[rest], h_s.at[0], h_r.at[0]).wait()
     ids = jnp.concatenate([asked[p] for p in range(n)], axis=1) - base
     idf = ids.astype(F32)
     up = jnp.floor((idf + 0.5) * (1.0 / 128))
@@ -440,63 +440,119 @@
     got = lax.dot_general(left, right, NT, preferred_element_type=F32)
     home[...] = got[:nb] + (got[nb:2 * nb] + got[2 * nb:])
 
-    def drain(jt, carry):
-        o_copy(jt).wait()
-        return carry
-
-    lax.fori_loop(0, nt, drain, 0)
-
-
-def run(n, count_products, count_consumers, fm, cols, chars, mean, tastes, coef, inv):
+    for t in range(max(nt - 5, 0), nt):
+        gather(t)
+    to_cons(PX, PR, px_s.at[0], px_r.at[0], partner).wait_send()
+    to_cons(YS, YR, y_s.at[0], y_r.at[0], across).wait_send()
+    to_cons(XO.at[:, mine], XO.at[:, mine], o_s.at[0], o_r.at[0], partner).wait_send()
+    pltpu.make_async_copy(XO, out, w_s.at[0]).wait()
+
+
+def run(n, count_products, count_consumers, fm, cols, chars, mean, tastes, coef):
     LP, K = chars.shape
     LI, W = tastes.shape[0], cols.shape[1]
-    block = inv.shape[1]
     half = W // 2
     cp = W // n
     room = -(-cp // 16) * 16
     pad = lanes(LP // n)
-    IC, WC, JT, GR = min(1024, LI), min(512, LI), min(512, LP), 32
+    IC, WC, JT, GR = min(1024, LI), min(512, LI), min(256, LP), 32
     nc, nt = LI // IC, LP // JT
     nb, pb = LP // 128, pad // 128
     dma = pltpu.SemaphoreType.DMA
     vm = pltpu.VMEM
     I32 = jnp.int32
+    ANY = pl.BlockSpec(memory_space=pltpu.HBM)
     return pl.pallas_call(
         functools.partial(
             step_kernel, n, cp, room, pad, float(count_products), float(count_consumers), IC, WC, JT, GR
         ),
         out_shape=(
             jax.ShapeDtypeStruct((LP, W), F32),
-            jax.ShapeDtypeStruct((LP // block, block), F32),
+            jax.ShapeDtypeStruct((1, LP), F32),
             jax.ShapeDtypeStruct((nb, 128), F32),
         ),
-        in_specs=[VMEM] * 7,
-        out_specs=(VMEM,) * 3,
+        in_specs=[VMEM, VMEM, ANY, VMEM, ANY, VMEM],
+        out_specs=(ANY, VMEM, VMEM),
         scratch_shapes=[
             vm((LP, 2 * K), BF16), vm((LI, 2 * K), BF16), vm((LP, 2 * K), BF16), vm((n * pad, 2 * K), BF16),
-            vm((LP // block, block, 2 * block), BF16), vm((1, LP), F32), vm((128, LP), BF16),
+            vm((1, LP), F32), vm((128, LP), BF16),
             vm((n, 1, pad), I32), vm((n, 1, pad), I32),
             vm((n, pad, K), BF16), vm((n, 1, pad), F32), vm((n, pad, K), BF16), vm((n, 1, pad), F32),
             vm((n, room, K), BF16), vm((1, W), F32), vm((n, room, K), BF16), vm((n, 1, W), F32),
             vm((cp, K), F32), vm((n, cp, K), F32),
             vm((LP, IC), F32), vm((n, nc, 2, IC), F32), vm((1, LI), F32), vm((1, LI), F32), vm((LI, W), BF16),
-            vm((JT, LI), F32), vm((JT, LI), BF16), vm((JT, 128), F32), vm((JT, 128), F32),
+            vm((LP, W), F32), vm((JT, LI), F32), vm((JT, LI), BF16), vm((JT, 128), F32), vm((JT, 128), F32),
             vm((LP, half), F32), vm((LP, half), F32), vm((LP, half), F32),
             vm((LP, half), BF16), vm((LP, half), BF16),
             vm((4, 1, LP), F32), vm((n, 1, pad), F32), vm((n, 1, pad), F32),
-        ] + [dma((n,))] * 14 + [dma((nc, n))] * 2 + [dma((nt,))] * 6 + [dma((4,))] * 2 + [dma((n,))] * 2,
+        ] + [dma((2,)), dma((1,)), dma((1,)), dma((n,)), dma((1,)), dma((n,))] + [dma((1,))] * 10
+        + [dma((nc,))] * 2 + [dma((1,)), dma((nt,))] * 3 + [dma((1,))] * 4,
         compiler_params=pltpu.CompilerParams(collective_id=1, has_side_effects=True, vmem_limit_bytes=LIMIT),
-    )(fm, cols, chars, mean, tastes, coef, inv)
+    )(fm, cols, chars, mean, tastes, coef)
+
+
+def firm_kernel(x, m, srow, home, out, mk, shares):
+    block = m.shape[1]
+    W = x.shape[1]
+    step = pl.program_id(0)
+
+    @pl.when(step == 0)
+    def _():
+        shares[...] = home[...]
+
+    for b in range(m.shape[0]):
+        rows = slice(b * block, (b + 1) * block)
+        mh = m[b].astype(BF16)
+        pair = jnp.concatenate([mh, (m[b] - mh.astype(F32)).astype(BF16)], axis=1)
+        v = x[rows, :]
+        h = v.astype(BF16)
+        both = jnp.concatenate([h, (v - h.astype(F32)).astype(BF16)], axis=1)
+        r = jnp.dot(pair, jnp.concatenate([both, both], axis=0), preferred_element_type=F32)
+        out[rows, :] = r[:, :W] + r[:, W:]
+        s = srow[:, rows]
+        s1 = s.astype(BF16).astype(F32)
+        left = jnp.concatenate([jnp.broadcast_to(s1, (8, block)), jnp.broadcast_to(s - s1, (8, block))], axis=0).astype(BF16)
+        g = lax.dot_general(jnp.concatenate([left, left], axis=1), pair, NT, preferred_element_type=F32)
+        mk[b:b + 1, :] = g[0:1] + g[8:9]
+
+
+def firms(x, inv, srow, home):
+    LP, W = x.shape
+    block = inv.shape[1]
+    per = min(8, inv.shape[0])
+    steps = inv.shape[0] // per
+    return pl.pallas_call(
+        firm_kernel,
+        grid=(steps,),
+        out_shape=(
+            jax.ShapeDtypeStruct((LP, W), F32),
+            jax.ShapeDtypeStruct((inv.shape[0], block), F32),
+            jax.ShapeDtypeStruct(home.shape, F32),
+        ),
+        in_specs=[
+            pl.BlockSpec((per * block, W), lambda i: (i, 0)),
+            pl.BlockSpec((per, block, block), lambda i: (i, 0, 0)),
+            pl.BlockSpec((1, per * block), lambda i: (0, i)),
+            pl.BlockSpec(home.shape, lambda i: (0, 0)),
+        ],
+        out_specs=(
+            pl.BlockSpec((per * block, W), lambda i: (i, 0)),
+            pl.BlockSpec((per, block), lambda i: (i, 0)),
+            pl.BlockSpec(home.shape, lambda i: (0, 0)),
+        ),
+        compiler_params=pltpu.CompilerParams(vmem_limit_bytes=LIMIT),
+    )(x, inv, srow, home)
 
 
 def body(tastes, price_coef, characteristics, mean_utility, panel_cols, firm_map, inverses):
     n = lax.axis_size("prod")
     LP = characteristics.shape[0]
-    response, markup, shares = run(
+    jacobian, srow, home = run(
         n, LP * n, tastes.shape[0] * lax.axis_size("cons"),
         firm_map[None, :], panel_cols[None, :], characteristics, mean_utility[None, :],
-        tastes, price_coef[None, :], inverses,
+        tastes, price_coef[None, :],
     )
+    response, markup, shares = firms(jacobian, inverses, srow, home)
     return shares.reshape(LP), markup.reshape(LP), response
 
 

time: 68.3 us -> 60.4 us (0.88)
  local copies, waits for them, and re-layouts: 5.63 us -> 0 us
  Pallas kernels: 61.8 us -> 59.5 us
    pallas_call x1, Pallas kernels: 61.8 us -> 56 us  [run(): pl.pallas_call(functools.partial(step_kernel, n, cp, room, pad, float(cou...]
    unnamed x3 -> x0, local copies, waits for them, and re-layouts: 5.63 us -> none
    pallas_call x0 -> x1, Pallas kernels: none -> 3.6 us  [firms(): pl.pallas_call(firm_kernel, grid=(steps,), out_shape=(jax.ShapeDtypeStruc...]
where the time goes in v2:
time: 60.4 us; the launch traced here: 60.2 us
  Pallas kernels  59.5 us (99%)
  between operations  0.64 us (1%)
    pallas_call x1, Pallas kernels, run(): pl.pallas_call(functools.partial(step_kernel, n, cp, room, pad, float(cou...  56 us
    pallas_call x1, Pallas kernels, firms(): pl.pallas_call(firm_kernel, grid=(steps,), out_shape=(jax.ShapeDtypeStruc...  3.6 us

profile of v2, /device:TPU:0, one launch (start us, length us, event | category | flops | bytes accessed | tf_op | source)
XLA Modules:
  0.0 60.2 jit_solution(10531603991741114442)
XLA Ops:
  0.6 56.0 %shard_map.94 = (f32[2048,256]{1,0:T(8,128)}, f32[1,2048]{1,0:T(1,128)}, f32[16,128]{1,0:T(8,128)}) custom-call(s32[1,2048]{1,0:T(1,128)} %bitcast.7, s32[1,256]{1,0:T(1,128)} %bitcast.9, bf16[2048,128]{1,0:T(8,128)(2,1)} %chars.1, f32[1,2048]{1,0:T(1,128)} %bitcast.8, bf16[4096,128]{1,0:T(8,128)(2,1)} %tastes.1, f32[1,4096]{1,0:T(1,128)} %bitcast.6), custom_call_target="tpu_custom_call" | custom-call | tf_op jit(solution)/shard_map/pallas_call | solution.py:465
  56.6 3.6 %shard_map.95 = (f32[2048,256]{1,0:T(8,128)}, f32[16,128]{1,0:T(8,128)}, f32[16,128]{1,0:T(8,128)}) custom-call(f32[2048,256]{1,0:T(8,128)} %get-tuple-element.9.x, f32[16,128,128]{2,1,0:T(8,128)} %m.1, f32[1,2048]{1,0:T(1,128)} %get-tuple-element.10.srow, f32[16,128]{1,0:T(8,128)} %get-tuple-element.11.home), custom_call_target="tpu_custom_call" | custom-call | tf_op jit(solution)/shard_map/pallas_call | solution.py:524

commit v3 on v2

--- a/solution.py
+++ b/solution.py
@@ -11,7 +11,7 @@
 NT = (((1,), (1,)), ((), ()))
 MESH = pl.DeviceIdType.MESH
 VMEM = pl.BlockSpec(memory_space=pltpu.VMEM)
-LIMIT = 63 * 1024 * 1024
+LIMIT = 48 * 1024 * 1024
 
 
 def lanes(count):
@@ -40,13 +40,14 @@
 
 def step_kernel(
     n, cp, room, pad, count_products, count_consumers, IC, WC, JT, GR,
-    fm, cols, chars, mean, tastes, coef,
+    fm_in, cols_in, chars, mean_in, tastes, coef_in,
     out, srow, home,
+    fm, cols, mean, coef,
     CA, TA, CF, TB, KEY, BT, sid, asked,
     X, XM, R, RM, XC, XCM, RC, RCM, CP, CC,
     UA, MS, PK, FV, WT,
-    XO, UB, SCB, SH, DG, PO, PX, PR, YS, YR, ST, SV, HV,
-    i_s, w_s, a_s, a_r, x_s, x_r, f_s, f_r, m_s, m_r, c_s, c_r, k_s, k_r, cc_s, cc_r,
+    UB, SCB, SH, DG, PO, PX, PR, YS, YR, ST, SV, HV,
+    i_s, a_s, a_r, x_s, x_r, f_s, f_r, g_s, g_r, m_s, m_r, c_s, c_r, k_s, k_r, cc_s, cc_r,
     ms_s, ms_r, px_s, px_r, y_s, y_r, o_s, o_r, st_s, st_r, h_s, h_r,
 ):
     me = lax.axis_index("prod")
@@ -89,10 +90,17 @@
     def to_cons(src, dst, s, r, peer):
         return pltpu.make_async_remote_copy(src, dst, s, r, device_id={"cons": peer}, device_id_type=MESH)
 
+    small = [
+        pltpu.make_async_copy(src, dst, i_s.at[2 + k])
+        for k, (src, dst) in enumerate(((fm_in, fm), (mean_in, mean), (cols_in, cols), (coef_in, coef)))
+    ]
+    for copy in small:
+        copy.start()
     load_chars = pltpu.make_async_copy(chars, CA.at[:, pl.ds(0, K)], i_s.at[0])
     load_tastes = pltpu.make_async_copy(tastes, TA.at[:, pl.ds(0, K)], i_s.at[1])
     load_chars.start()
     load_tastes.start()
+    small[0].wait()
 
     fmf = fm[...].astype(F32)
     source = jnp.floor((fmf + 0.5) * (1.0 / LP))
@@ -135,17 +143,20 @@
         for b in range(pb):
             sid[p, :, b * 128:(b + 1) * 128] = wanted[p * pb + b:p * pb + b + 1]
 
-    pl.semaphore_wait(barrier, n + 2)
-
-    def a_copy(d):
-        return to_prod(sid.at[lax.rem(me + d, n)], asked.at[me], a_s.at[0], a_r.at[d], d)
-
-    loop(lambda d: a_copy(d).start())
-    asked[me] = sid[me]
-
+    small[1].wait()
     for g in range(nb):
         CA[g * 128:(g + 1) * 128, K:] = split(turned(mean[:, g * 128:(g + 1) * 128]), K)
     TA[:, K:] = jnp.where(lax.broadcasted_iota(jnp.int32, (LI, K), 1) < 3, 1.0, 0.0).astype(BF16)
+    pl.semaphore_wait(barrier, n + 2)
+
+    def a_copy(d):
+        return to_prod(sid.at[lax.rem(me + d, n)], asked.at[me], a_s.at[0], a_r.at[d], d)
+
+    loop(lambda d: a_copy(d).start())
+    asked[me] = sid[me]
+
+    small[2].wait()
+    small[3].wait()
     load_chars.wait()
 
     def pick(wants):
@@ -196,8 +207,12 @@
     def cc_copy(d):
         return to_prod(CP, CC.at[me], cc_s.at[0], cc_r.at[0], d)
 
-    span = pad // 2
-    part = pl.ds(pl.multiple_of(core * span, span), span)
+    span = pad // 4
+
+    def quarter(c):
+        return pl.ds(pl.multiple_of(c * span, span), span)
+
+    part, other = quarter(cons), quarter(across)
 
     def x_copy(d):
         return to_prod(X.at[lax.rem(me + d, n), part], R.at[me, part], x_s.at[0], x_r.at[d], d)
@@ -205,12 +220,41 @@
     def m_copy(d):
         return to_prod(XM.at[lax.rem(me + d, n)], RM.at[me], m_s.at[0], m_r.at[0], d)
 
-    def f_copy(d):
+    def g_copy(d):
         src = lax.rem(me + n - d, n)
-        return to_cons(R.at[src, part], R.at[src, part], f_s.at[0], f_r.at[0], partner)
+        return to_cons(R.at[src, part], R.at[src, part], g_s.at[0], g_r.at[0], across)
+
+    def f_copy(d, which):
+        src = lax.rem(me + n - d, n)
+        return to_cons(R.at[src, which], R.at[src, which], f_s.at[0], f_r.at[0], partner)
 
     load_tastes.wait()
     lax.fori_loop(0, 1, stats, 0)
+    def answer(k, carry):
+        sources = [lax.rem(me + n - 2 * k - h, n) for h in range(2)]
+
+        @pl.when(k > 0)
+        def _():
+            a_copy(2 * k).wait_recv()
+
+        a_copy(2 * k + 1).wait_recv()
+        rows, means = pick([asked[src, :, b * 128:(b + 1) * 128] for src in sources for b in range(pb)])
+        for h, src in enumerate(sources):
+            X[src] = rows[h * pad:(h + 1) * pad]
+            for b in range(pb):
+                XM[src, :, b * 128:(b + 1) * 128] = means[h * pb + b]
+
+        @pl.when(k > 0)
+        def _():
+            x_copy(n - 2 * k).start()
+            m_copy(n - 2 * k).start()
+
+        x_copy(n - 2 * k - 1).start()
+        m_copy(n - 2 * k - 1).start()
+        return carry
+
+    lax.fori_loop(0, n // 2, answer, 0)
+    all_of(sid.at[rest], a_s.at[0], a_r.at[0]).wait_send()
     all_of(RC.at[rest], c_s.at[0], c_r.at[0]).wait()
     all_of(RCM.at[rest], k_s.at[0], k_r.at[0]).wait()
     total = RC[0, :cp, :].astype(F32)
@@ -222,68 +266,18 @@
     loop(lambda d: cc_copy(d).start())
     CC[me] = CP[...]
 
-    def answer(k, carry):
-        sources = [lax.rem(me + n - 2 * k - h, n) for h in range(2)]
-
-        @pl.when(k > 0)
-        def _():
-            a_copy(2 * k).wait_recv()
-
-        a_copy(2 * k + 1).wait_recv()
-        rows, means = pick([asked[src, :, b * 128:(b + 1) * 128] for src in sources for b in range(pb)])
-        for h, src in enumerate(sources):
-            X[src] = rows[h * pad:(h + 1) * pad]
-            for b in range(pb):
-                XM[src, :, b * 128:(b + 1) * 128] = means[h * pb + b]
-
-        @pl.when(k > 0)
-        def _():
-            x_copy(n - 2 * k).start()
-            m_copy(n - 2 * k).start()
-
-        x_copy(n - 2 * k - 1).start()
-        m_copy(n - 2 * k - 1).start()
-        return carry
-
-    lax.fori_loop(0, n // 2, answer, 0)
-    all_of(sid.at[rest], a_s.at[0], a_r.at[0]).wait_send()
     R[me] = X[me]
     RM[me] = XM[me]
-    lax.fori_loop(1, nc, stats, 0)
+    held = max(nc - 1, 1)
+    lax.fori_loop(1, held, stats, 0)
 
     def relay(d):
         x_copy(d).wait_recv()
-        f_copy(d).start()
+        g_copy(d).start()
+        f_copy(d, part).start()
 
     loop(relay)
-    all_of(X.at[rest, part], x_s.at[0], x_r.at[0]).wait_send()
-
-    all_of(RM.at[rest], m_s.at[0], m_r.at[0]).wait()
-    all_of(R.at[rest, part], f_s.at[0], f_r.at[0]).wait()
-
-    for p in range(n):
-        TB[p * pad:(p + 1) * pad, :K] = R[p]
-        for b in range(pb):
-            at = p * pad + b * 128
-            TB[at:at + 128, K:] = split(turned(RM[p, :, b * 128:(b + 1) * 128]), K)
-
-    def firm(g, carry):
-        bands = []
-        for h in range(8):
-            rows = pl.ds(pl.multiple_of(g * 1024 + h * 128, 128), 128)
-            want = turned(fm[:, rows].astype(F32))
-            bands.append(jnp.concatenate(
-                [
-                    jnp.where(want == sid[p, :, b * 128:(b + 1) * 128].astype(F32), 1.0, 0.0).astype(BF16)
-                    for p in range(n) for b in range(pb)
-                ],
-                axis=1,
-            ))
-        rows = pl.ds(pl.multiple_of(g * 1024, 1024), 1024)
-        CF[rows, :] = jnp.dot(jnp.concatenate(bands, axis=0), TB[...], preferred_element_type=F32).astype(BF16)
-        return carry
-
-    lax.fori_loop(0, LP // 1024, firm, 0)
+    lax.fori_loop(held, nc, stats, 0)
 
     all_of(CC.at[rest], cc_s.at[0], cc_r.at[0]).wait()
     ccv = CC[...].reshape(n * cp, K).astype(BF16)
@@ -311,7 +305,42 @@
         weights(ic)
         return carry
 
-    lax.fori_loop(0, nc, weights_step, 0)
+    early = max(held - 1, 0)
+    lax.fori_loop(0, early, weights_step, 0)
+    all_of(R.at[rest, part], g_s.at[0], g_r.at[0]).wait()
+    loop(lambda d: f_copy(d, other).start())
+    all_of(X.at[rest, part], x_s.at[0], x_r.at[0]).wait_send()
+    lax.fori_loop(early, held, weights_step, 0)
+
+    all_of(RM.at[rest], m_s.at[0], m_r.at[0]).wait()
+    all_of(R.at[rest, pl.ds(0, 2 * span)], f_s.at[0], f_r.at[0]).wait()
+
+    for p in range(n):
+        TB[p * pad:(p + 1) * pad, :K] = R[p]
+        for b in range(pb):
+            at = p * pad + b * 128
+            TB[at:at + 128, K:] = split(turned(RM[p, :, b * 128:(b + 1) * 128]), K)
+
+    def firm(g, carry):
+        bands = []
+        for h in range(8):
+            rows = pl.ds(pl.multiple_of(g * 1024 + h * 128, 128), 128)
+            want = turned(fm[:, rows].astype(F32))
+            bands.append(jnp.concatenate(
+                [
+                    jnp.where(want == sid[p, :, b * 128:(b + 1) * 128].astype(F32), 1.0, 0.0).astype(BF16)
+                    for p in range(n) for b in range(pb)
+                ],
+                axis=1,
+            ))
+        rows = pl.ds(pl.multiple_of(g * 1024, 1024), 1024)
+        CF[rows, :] = jnp.dot(jnp.concatenate(bands, axis=0), TB[...], preferred_element_type=F32).astype(BF16)
+        return carry
+
+    lax.fori_loop(0, LP // 1024, firm, 0)
+
+    lax.fori_loop(held, nc, weights_step, 0)
+
 
     def tile_rows(jt):
         return pl.ds(pl.multiple_of(jt * JT, JT), JT)
@@ -328,13 +357,7 @@
 
     def o_copy(jt):
         rows = tile_rows(jt)
-        return to_cons(XO.at[rows, mine], XO.at[rows, mine], o_s.at[0], o_r.at[jt], partner)
-
-    theirs = pl.ds(pl.multiple_of((1 - core) * half, half), half)
-
-    def write(jt, which):
-        rows = tile_rows(jt)
-        return pltpu.make_async_copy(XO.at[rows, which], out.at[rows, which], w_s.at[0])
+        return to_cons(out.at[rows, mine], out.at[rows, mine], o_s.at[0], o_r.at[jt], partner)
 
     def st_copy(d, jt):
         rows = tile_rows(jt)
@@ -351,13 +374,11 @@
     def finish(jt):
         y_copy(jt).wait_recv()
         rows = tile_rows(jt)
-        XO[rows, mine] = (YS[rows, :].astype(F32) + YR[rows, :].astype(F32)) / count_consumers
+        out[rows, mine] = (YS[rows, :].astype(F32) + YR[rows, :].astype(F32)) / count_consumers
         o_copy(jt).start()
-        write(jt, mine).start()
 
     def gather(jt):
         o_copy(jt).wait_recv()
-        write(jt, theirs).start()
 
     heads_row = cols[...].astype(F32)
 
@@ -410,7 +431,10 @@
 
     lax.fori_loop(0, nt, panel, 0)
     forward(nt - 1)
-
+    idf = (jnp.concatenate([asked[p] for p in range(n)], axis=1) - base).astype(F32)
+    up = jnp.floor((idf + 0.5) * (1.0 / 128))
+    right = jnp.where(idf - up * 128.0 == rows_of((128, n * pad)), 1.0, 0.0).astype(BF16)
+    mask = up == rows_of((nb, n * pad))
     all_of(ST.at[pl.ds(0, 3)], st_s.at[0], st_r.at[0]).wait()
     share = (ST[0] + ST[1] + ST[2] + ST[3]) / count_consumers
     sums = scatter(thirds(share))
@@ -424,28 +448,19 @@
 
     loop(lambda d: h_copy(d).start())
     HV[me] = SV[me]
-    for t in range(max(nt - 4, 0), nt - 1):
+    srow[...] = share
+    for t in range(max(nt - 4, 0), nt):
         finish(t)
-    srow[...] = share
-    finish(nt - 1)
-
+    for t in range(max(nt - 5, 0), nt):
+        gather(t)
     all_of(HV.at[rest], h_s.at[0], h_r.at[0]).wait()
-    ids = jnp.concatenate([asked[p] for p in range(n)], axis=1) - base
-    idf = ids.astype(F32)
-    up = jnp.floor((idf + 0.5) * (1.0 / 128))
-    right = jnp.where(idf - up * 128.0 == rows_of((128, n * pad)), 1.0, 0.0).astype(BF16)
-    mask = up == rows_of((nb, n * pad))
     back = jnp.concatenate([HV[p] for p in range(n)], axis=1)
     left = jnp.concatenate([jnp.where(mask, p, 0.0) for p in thirds(back)], axis=0).astype(BF16)
     got = lax.dot_general(left, right, NT, preferred_element_type=F32)
     home[...] = got[:nb] + (got[nb:2 * nb] + got[2 * nb:])
-
-    for t in range(max(nt - 5, 0), nt):
-        gather(t)
     to_cons(PX, PR, px_s.at[0], px_r.at[0], partner).wait_send()
     to_cons(YS, YR, y_s.at[0], y_r.at[0], across).wait_send()
-    to_cons(XO.at[:, mine], XO.at[:, mine], o_s.at[0], o_r.at[0], partner).wait_send()
-    pltpu.make_async_copy(XO, out, w_s.at[0]).wait()
+    to_cons(out.at[:, mine], out.at[:, mine], o_s.at[0], o_r.at[0], partner).wait_send()
 
 
 def run(n, count_products, count_consumers, fm, cols, chars, mean, tastes, coef):
@@ -471,9 +486,10 @@
             jax.ShapeDtypeStruct((1, LP), F32),
             jax.ShapeDtypeStruct((nb, 128), F32),
         ),
-        in_specs=[VMEM, VMEM, ANY, VMEM, ANY, VMEM],
-        out_specs=(ANY, VMEM, VMEM),
+        in_specs=[ANY] * 6,
+        out_specs=(VMEM,) * 3,
         scratch_shapes=[
+            vm((1, LP), I32), vm((1, W), I32), vm((1, LP), F32), vm((1, LI), F32),
             vm((LP, 2 * K), BF16), vm((LI, 2 * K), BF16), vm((LP, 2 * K), BF16), vm((n * pad, 2 * K), BF16),
             vm((1, LP), F32), vm((128, LP), BF16),
             vm((n, 1, pad), I32), vm((n, 1, pad), I32),
@@ -481,14 +497,14 @@
             vm((n, room, K), BF16), vm((1, W), F32), vm((n, room, K), BF16), vm((n, 1, W), F32),
             vm((cp, K), F32), vm((n, cp, K), F32),
             vm((LP, IC), F32), vm((n, nc, 2, IC), F32), vm((1, LI), F32), vm((1, LI), F32), vm((LI, W), BF16),
-            vm((LP, W), F32), vm((JT, LI), F32), vm((JT, LI), BF16), vm((JT, 128), F32), vm((JT, 128), F32),
+            vm((JT, LI), F32), vm((JT, LI), BF16), vm((JT, 128), F32), vm((JT, 128), F32),
             vm((LP, half), F32), vm((LP, half), F32), vm((LP, half), F32),
             vm((LP, half), BF16), vm((LP, half), BF16),
             vm((4, 1, LP), F32), vm((n, 1, pad), F32), vm((n, 1, pad), F32),
-        ] + [dma((2,)), dma((1,)), dma((1,)), dma((n,)), dma((1,)), dma((n,))] + [dma((1,))] * 10
+        ] + [dma((6,)), dma((1,)), dma((n,)), dma((1,)), dma((n,))] + [dma((1,))] * 12
         + [dma((nc,))] * 2 + [dma((1,)), dma((nt,))] * 3 + [dma((1,))] * 4,
         compiler_params=pltpu.CompilerParams(collective_id=1, has_side_effects=True, vmem_limit_bytes=LIMIT),
-    )(fm, cols, chars, mean, tastes, coef)
+    )(*[pltpu.with_memory_space_constraint(v, pltpu.HBM) for v in (fm, cols, chars, mean, tastes, coef)])
 
 
 def firm_kernel(x, m, srow, home, out, mk, shares):
@@ -513,7 +529,7 @@
         s1 = s.astype(BF16).astype(F32)
         left = jnp.concatenate([jnp.broadcast_to(s1, (8, block)), jnp.broadcast_to(s - s1, (8, block))], axis=0).astype(BF16)
         g = lax.dot_general(jnp.concatenate([left, left], axis=1), pair, NT, preferred_element_type=F32)
-        mk[b:b + 1, :] = g[0:1] + g[8:9]
+        mk[pl.ds(step * m.shape[0] + b, 1), :] = g[0:1] + g[8:9]
 
 
 def firms(x, inv, srow, home):
@@ -537,10 +553,10 @@
         ],
         out_specs=(
             pl.BlockSpec((per * block, W), lambda i: (i, 0)),
-            pl.BlockSpec((per, block), lambda i: (i, 0)),
+            pl.BlockSpec((inv.shape[0], block), lambda i: (0, 0)),
             pl.BlockSpec(home.shape, lambda i: (0, 0)),
         ),
-        compiler_params=pltpu.CompilerParams(vmem_limit_bytes=LIMIT),
+        compiler_params=pltpu.CompilerParams(vmem_limit_bytes=16 * 1024 * 1024),
     )(x, inv, srow, home)
 
 

time: 60.4 us -> 54.7 us (0.906)
  Pallas kernels: 59.5 us -> 53.9 us
    pallas_call x1, Pallas kernels: 56 us -> 51.7 us  [run(): pl.pallas_call(functools.partial(step_kernel, n, cp, room, pad, float(cou...]
    pallas_call x1, Pallas kernels: 3.6 us -> 2.19 us  [firms(): pl.pallas_call(firm_kernel, grid=(steps,), out_shape=(jax.ShapeDtypeStruc...]
where the time goes in v3:
time: 54.7 us; the launch traced here: 54.6 us
  Pallas kernels  53.9 us (99%)
  between operations  0.66 us (1%)
    pallas_call x1, Pallas kernels, run(): pl.pallas_call(functools.partial(step_kernel, n, cp, room, pad, float(cou...  51.7 us
    pallas_call x1, Pallas kernels, firms(): pl.pallas_call(firm_kernel, grid=(steps,), out_shape=(jax.ShapeDtypeStruc...  2.19 us

profile of v3, /device:TPU:0, one launch (start us, length us, event | category | flops | bytes accessed | tf_op | source)
XLA Modules:
  0.0 54.6 jit_solution(14802395774895706860)
XLA Ops:
  0.6 0.0 copy-start
  0.6 51.7 %shard_map.94 = (f32[2048,256]{1,0:T(8,128)S(1)}, f32[1,2048]{1,0:T(1,128)S(1)}, f32[16,128]{1,0:T(8,128)S(1)}) custom-call(s32[1,2048]{1,0:T(1,128)} %bitcast.7, s32[1,256]{1,0:T(1,128)} %bitcast.9, bf16[2048,128]{1,0:T(8,128)(2,1)} %chars.1, f32[1,2048]{1,0:T(1,128)} %bitcast.8, bf16[4096,128]{1,0:T(8,128)(2,1)} %tastes.1, f32[1,4096]{1,0:T(1,128)} %bitcast.6), custom_call_target="tpu_custom_call" | custom-call | tf_op jit(solution)/shard_map/pallas_call | solution.py:480
  52.4 0.0 copy-done
  52.4 2.2 %shard_map.95 = (f32[2048,256]{1,0:T(8,128)}, f32[16,128]{1,0:T(8,128)}, f32[16,128]{1,0:T(8,128)}) custom-call(f32[2048,256]{1,0:T(8,128)S(1)} %get-tuple-element.9.x, f32[16,128,128]{2,1,0:T(8,128)S(1)} %copy-done, f32[1,2048]{1,0:T(1,128)S(1)} %get-tuple-element.10.srow, f32[16,128]{1,0:T(8,128)S(1)} %get-tuple-element.11.home), custom_call_target="tpu_custom_call" | custom-call | tf_op jit(solution)/shard_map/pallas_call | solution.py:540
Async XLA Ops:
  0.6 51.7 %copy-start = (f32[16,128,128]{2,1,0:T(8,128)S(1)}, f32[16,128,128]{2,1,0:T(8,128)}, u32[]{:S(2)}) copy-start(f32[16,128,128]{2,1,0:T(8,128)} %m.1) | copy-start | bytes 3145732

commit v4 on v3

--- a/solution.py
+++ b/solution.py
@@ -40,11 +40,11 @@
 
 def step_kernel(
     n, cp, room, pad, count_products, count_consumers, IC, WC, JT, GR,
-    fm_in, cols_in, chars, mean_in, tastes, coef_in,
-    out, srow, home,
-    fm, cols, mean, coef,
+    fm_in, cols_in, chars, mean_in, tastes, coef_in, inv_in,
+    out, pairs, mk, home,
+    fm, cols, mean, coef, inv,
     CA, TA, CF, TB, KEY, BT, sid, asked,
-    X, XM, R, RM, XC, XCM, RC, RCM, CP, CC,
+    IDC, RT, UP, X, XM, R, RM, XC, XCM, RC, RCM, CP, CC,
     UA, MS, PK, FV, WT,
     UB, SCB, SH, DG, PO, PX, PR, YS, YR, ST, SV, HV,
     i_s, a_s, a_r, x_s, x_r, f_s, f_r, g_s, g_r, m_s, m_r, c_s, c_r, k_s, k_r, cc_s, cc_r,
@@ -59,6 +59,7 @@
     LI = tastes.shape[0]
     W = cols.shape[1]
     half = W // 2
+    block = inv.shape[1]
     pp = LP // n
     nb, pb = LP // 128, pad // 128
     nc, nw, nt = LI // IC, LI // WC, LP // JT
@@ -100,6 +101,8 @@
     load_tastes = pltpu.make_async_copy(tastes, TA.at[:, pl.ds(0, K)], i_s.at[1])
     load_chars.start()
     load_tastes.start()
+    load_inv = pltpu.make_async_copy(inv_in, inv, i_s.at[6])
+    load_inv.start()
     small[0].wait()
 
     fmf = fm[...].astype(F32)
@@ -215,14 +218,14 @@
     part, other = quarter(cons), quarter(across)
 
     def x_copy(d):
-        return to_prod(X.at[lax.rem(me + d, n), part], R.at[me, part], x_s.at[0], x_r.at[d], d)
+        return to_prod(X.at[lax.rem(me + d, n)], R.at[me, part], x_s.at[0], x_r.at[d], d)
 
     def m_copy(d):
         return to_prod(XM.at[lax.rem(me + d, n)], RM.at[me], m_s.at[0], m_r.at[0], d)
 
-    def g_copy(d):
+    def g_copy(d, batch):
         src = lax.rem(me + n - d, n)
-        return to_cons(R.at[src, part], R.at[src, part], g_s.at[0], g_r.at[0], across)
+        return to_cons(R.at[src, part], R.at[src, part], g_s.at[0], g_r.at[batch], across)
 
     def f_copy(d, which):
         src = lax.rem(me + n - d, n)
@@ -230,30 +233,34 @@
 
     load_tastes.wait()
     lax.fori_loop(0, 1, stats, 0)
-    def answer(k, carry):
-        sources = [lax.rem(me + n - 2 * k - h, n) for h in range(2)]
-
-        @pl.when(k > 0)
-        def _():
-            a_copy(2 * k).wait_recv()
-
-        a_copy(2 * k + 1).wait_recv()
-        rows, means = pick([asked[src, :, b * 128:(b + 1) * 128] for src in sources for b in range(pb)])
-        for h, src in enumerate(sources):
-            X[src] = rows[h * pad:(h + 1) * pad]
-            for b in range(pb):
-                XM[src, :, b * 128:(b + 1) * 128] = means[h * pb + b]
-
-        @pl.when(k > 0)
-        def _():
-            x_copy(n - 2 * k).start()
-            m_copy(n - 2 * k).start()
-
-        x_copy(n - 2 * k - 1).start()
-        m_copy(n - 2 * k - 1).start()
-        return carry
-
-    lax.fori_loop(0, n // 2, answer, 0)
+    loop(lambda d: a_copy(d).wait_recv())
+    for p in range(n):
+        for b in range(pb):
+            IDC[p, b * 128:(b + 1) * 128, :] = turned((asked[p, :, b * 128:(b + 1) * 128] - base).astype(F32))
+    spot = lax.broadcasted_iota(jnp.int32, (1, 128), 1).astype(F32)
+
+    def hots(want):
+        return jnp.concatenate(
+            [jnp.where(want == spot + float(b * 128), 1.0, 0.0).astype(BF16) for b in range(nb)], axis=1
+        )
+
+    asks = jnp.concatenate([hots(IDC[p, part, :]) for p in range(n)] + [hots(IDC[me])], axis=0)
+    got = jnp.dot(asks, CA[:, :K], preferred_element_type=F32).astype(BF16)
+    for p in range(n):
+        X[p] = got[p * span:(p + 1) * span]
+    R[me] = got[n * span:]
+    loop(lambda d: x_copy(d).start())
+    idf = (jnp.concatenate([asked[p] for p in range(n)], axis=1) - base).astype(F32)
+    up = jnp.floor((idf + 0.5) * (1.0 / 128))
+    RT[...] = jnp.where(idf - up * 128.0 == rows_of((128, n * pad)), 1.0, 0.0).astype(BF16)
+    UP[...] = up
+    grid = jnp.concatenate([mean[:, b * 128:(b + 1) * 128] for b in range(nb)], axis=0)
+    found = jnp.dot(jnp.concatenate(thirds(grid), axis=0).astype(BF16), RT[...], preferred_element_type=F32)
+    found = found[:nb] + (found[nb:2 * nb] + found[2 * nb:])
+    means = jnp.sum(jnp.where(up == rows_of((nb, n * pad)), found, 0.0), axis=0, keepdims=True)
+    for p in range(n):
+        XM[p] = means[:, p * pad:(p + 1) * pad]
+    loop(lambda d: m_copy(d).start())
     all_of(sid.at[rest], a_s.at[0], a_r.at[0]).wait_send()
     all_of(RC.at[rest], c_s.at[0], c_r.at[0]).wait()
     all_of(RCM.at[rest], k_s.at[0], k_r.at[0]).wait()
@@ -262,25 +269,41 @@
     for p in range(1, n):
         total = total + RC[p, :cp, :].astype(F32)
         heads = heads + RCM[p]
-    CP[...] = total
+    CP[:cp, :] = total.astype(BF16)
     loop(lambda d: cc_copy(d).start())
     CC[me] = CP[...]
 
-    R[me] = X[me]
     RM[me] = XM[me]
     held = max(nc - 1, 1)
     lax.fori_loop(1, held, stats, 0)
 
-    def relay(d):
-        x_copy(d).wait_recv()
-        g_copy(d).start()
-        f_copy(d, part).start()
-
-    loop(relay)
+    first = n // 2
+
+    def pass_on(batch, lo, hi):
+        def step(d, carry):
+            x_copy(d).wait_recv()
+            f_copy(d, part).start()
+            return carry
+        lax.fori_loop(lo, hi, step, 0)
+        def across_step(d, carry):
+            g_copy(d, batch).start()
+            return carry
+        lax.fori_loop(lo, hi, across_step, 0)
+
+    def hand_over(batch, lo, hi):
+        all_of(R.at[pl.ds(0, hi - lo), part], g_s.at[0], g_r.at[batch]).wait_recv()
+        def step(d, carry):
+            f_copy(d, other).start()
+            return carry
+        lax.fori_loop(lo, hi, step, 0)
+
+    pass_on(0, 1, first)
+    pass_on(1, first, n)
     lax.fori_loop(held, nc, stats, 0)
+    hand_over(0, 1, first)
 
     all_of(CC.at[rest], cc_s.at[0], cc_r.at[0]).wait()
-    ccv = CC[...].reshape(n * cp, K).astype(BF16)
+    ccv = CC[:, :cp, :].astype(F32).reshape(n * cp, K).astype(BF16)
     cm = jnp.concatenate([turned(heads[:, g * 128:(g + 1) * 128])[:, :1] for g in range(W // 128)], axis=0)
 
     def weights(ic):
@@ -305,21 +328,21 @@
         weights(ic)
         return carry
 
-    early = max(held - 1, 0)
-    lax.fori_loop(0, early, weights_step, 0)
-    all_of(R.at[rest, part], g_s.at[0], g_r.at[0]).wait()
-    loop(lambda d: f_copy(d, other).start())
-    all_of(X.at[rest, part], x_s.at[0], x_r.at[0]).wait_send()
-    lax.fori_loop(early, held, weights_step, 0)
+    lax.fori_loop(0, min(1, held), weights_step, 0)
+    hand_over(1, first, n)
+    lax.fori_loop(min(1, held), held, weights_step, 0)
+    all_of(R.at[rest, part], g_s.at[0], g_r.at[0]).wait_send()
+    all_of(X.at[rest], x_s.at[0], x_r.at[0]).wait_send()
 
     all_of(RM.at[rest], m_s.at[0], m_r.at[0]).wait()
-    all_of(R.at[rest, pl.ds(0, 2 * span)], f_s.at[0], f_r.at[0]).wait()
-
     for p in range(n):
-        TB[p * pad:(p + 1) * pad, :K] = R[p]
         for b in range(pb):
             at = p * pad + b * 128
             TB[at:at + 128, K:] = split(turned(RM[p, :, b * 128:(b + 1) * 128]), K)
+    all_of(R.at[rest, pl.ds(0, 2 * span)], f_s.at[0], f_r.at[0]).wait()
+
+    for p in range(n):
+        TB[p * pad:(p + 1) * pad, :K] = R[p]
 
     def firm(g, carry):
         bands = []
@@ -353,11 +376,11 @@
         rows = tile_rows(jt)
         return to_cons(YS.at[rows], YR.at[rows], y_s.at[0], y_r.at[jt], across)
 
-    mine = pl.ds(pl.multiple_of(core * half, half), half)
-
-    def o_copy(jt):
+    mine = [pl.ds(pl.multiple_of(core * half + k * W, half), half) for k in range(2)]
+
+    def o_copy(jt, k):
         rows = tile_rows(jt)
-        return to_cons(out.at[rows, mine], out.at[rows, mine], o_s.at[0], o_r.at[jt], partner)
+        return to_cons(out.at[rows, mine[k]], out.at[rows, mine[k]], o_s.at[0], o_r.at[jt], partner)
 
     def st_copy(d, jt):
         rows = tile_rows(jt)
@@ -374,11 +397,16 @@
     def finish(jt):
         y_copy(jt).wait_recv()
         rows = tile_rows(jt)
-        out[rows, mine] = (YS[rows, :].astype(F32) + YR[rows, :].astype(F32)) / count_consumers
-        o_copy(jt).start()
+        x = (YS[rows, :].astype(F32) + YR[rows, :].astype(F32)) / count_consumers
+        h = x.astype(BF16)
+        out[rows, mine[0]] = h
+        out[rows, mine[1]] = (x - h.astype(F32)).astype(BF16)
+        o_copy(jt, 0).start()
+        o_copy(jt, 1).start()
 
     def gather(jt):
-        o_copy(jt).wait_recv()
+        both = out.at[tile_rows(jt), pl.ds(0, W)]
+        to_cons(both, both, o_s.at[0], o_r.at[jt], partner).wait_recv()
 
     heads_row = cols[...].astype(F32)
 
@@ -399,8 +427,6 @@
             DG[band, :] = dg
         acc = jnp.dot(SCB[...], WT[...], preferred_element_type=F32)
         ST[cons, 0:1, rows] = jnp.sum(SH[...].T, axis=0, keepdims=True)
-        for d in range(1, 4):
-            st_copy(d, jt).start()
         diag = jnp.sum(DG[...], axis=1, keepdims=True)
         ids = jnp.concatenate(
             [
@@ -414,6 +440,8 @@
         PO[rows, :] = jnp.where(core == 0, first, second)
         PX[rows, :] = jnp.where(core == 0, second, first)
         px_copy(jt).start()
+        for d in range(1, 4):
+            st_copy(d, jt).start()
 
         @pl.when(jt > 0)
         def _():
@@ -431,10 +459,6 @@
 
     lax.fori_loop(0, nt, panel, 0)
     forward(nt - 1)
-    idf = (jnp.concatenate([asked[p] for p in range(n)], axis=1) - base).astype(F32)
-    up = jnp.floor((idf + 0.5) * (1.0 / 128))
-    right = jnp.where(idf - up * 128.0 == rows_of((128, n * pad)), 1.0, 0.0).astype(BF16)
-    mask = up == rows_of((nb, n * pad))
     all_of(ST.at[pl.ds(0, 3)], st_s.at[0], st_r.at[0]).wait()
     share = (ST[0] + ST[1] + ST[2] + ST[3]) / count_consumers
     sums = scatter(thirds(share))
@@ -448,22 +472,36 @@
 
     loop(lambda d: h_copy(d).start())
     HV[me] = SV[me]
-    srow[...] = share
+    load_inv.wait()
+    s1 = share.astype(BF16).astype(F32)
+    s2 = share - s1
+    for b in range(inv.shape[0]):
+        m = inv[b]
+        mh = m.astype(BF16)
+        pair = jnp.concatenate([mh, (m - mh.astype(F32)).astype(BF16)], axis=1)
+        pairs[b] = pair
+        at = slice(b * block, (b + 1) * block)
+        left = jnp.concatenate(
+            [jnp.broadcast_to(s1[:, at], (8, block)), jnp.broadcast_to(s2[:, at], (8, block))], axis=0
+        ).astype(BF16)
+        g = lax.dot_general(jnp.concatenate([left, left], axis=1), pair, NT, preferred_element_type=F32)
+        mk[b:b + 1, :] = g[0:1] + g[8:9]
     for t in range(max(nt - 4, 0), nt):
         finish(t)
     for t in range(max(nt - 5, 0), nt):
         gather(t)
     all_of(HV.at[rest], h_s.at[0], h_r.at[0]).wait()
     back = jnp.concatenate([HV[p] for p in range(n)], axis=1)
+    mask = UP[...] == rows_of((nb, n * pad))
     left = jnp.concatenate([jnp.where(mask, p, 0.0) for p in thirds(back)], axis=0).astype(BF16)
-    got = lax.dot_general(left, right, NT, preferred_element_type=F32)
+    got = lax.dot_general(left, RT[...], NT, preferred_element_type=F32)
     home[...] = got[:nb] + (got[nb:2 * nb] + got[2 * nb:])
     to_cons(PX, PR, px_s.at[0], px_r.at[0], partner).wait_send()
     to_cons(YS, YR, y_s.at[0], y_r.at[0], across).wait_send()
-    to_cons(out.at[:, mine], out.at[:, mine], o_s.at[0], o_r.at[0], partner).wait_send()
-
-
-def run(n, count_products, count_consumers, fm, cols, chars, mean, tastes, coef):
+    to_cons(out.at[:, pl.ds(0, W)], out.at[:, pl.ds(0, W)], o_s.at[0], o_r.at[0], partner).wait_send()
+
+
+def run(n, count_products, count_consumers, fm, cols, chars, mean, tastes, coef, inv):
     LP, K = chars.shape
     LI, W = tastes.shape[0], cols.shape[1]
     half = W // 2
@@ -473,6 +511,7 @@
     IC, WC, JT, GR = min(1024, LI), min(512, LI), min(256, LP), 32
     nc, nt = LI // IC, LP // JT
     nb, pb = LP // 128, pad // 128
+    count, block = inv.shape[0], inv.shape[1]
     dma = pltpu.SemaphoreType.DMA
     vm = pltpu.VMEM
     I32 = jnp.int32
@@ -482,93 +521,82 @@
             step_kernel, n, cp, room, pad, float(count_products), float(count_consumers), IC, WC, JT, GR
         ),
         out_shape=(
-            jax.ShapeDtypeStruct((LP, W), F32),
-            jax.ShapeDtypeStruct((1, LP), F32),
+            jax.ShapeDtypeStruct((LP, 2 * W), BF16),
+            jax.ShapeDtypeStruct((count, block, 2 * block), BF16),
+            jax.ShapeDtypeStruct((count, block), F32),
             jax.ShapeDtypeStruct((nb, 128), F32),
         ),
-        in_specs=[ANY] * 6,
-        out_specs=(VMEM,) * 3,
+        in_specs=[ANY] * 7,
+        out_specs=(VMEM,) * 4,
         scratch_shapes=[
-            vm((1, LP), I32), vm((1, W), I32), vm((1, LP), F32), vm((1, LI), F32),
+            vm((1, LP), I32), vm((1, W), I32), vm((1, LP), F32), vm((1, LI), F32), vm(inv.shape, F32),
             vm((LP, 2 * K), BF16), vm((LI, 2 * K), BF16), vm((LP, 2 * K), BF16), vm((n * pad, 2 * K), BF16),
             vm((1, LP), F32), vm((128, LP), BF16),
             vm((n, 1, pad), I32), vm((n, 1, pad), I32),
-            vm((n, pad, K), BF16), vm((n, 1, pad), F32), vm((n, pad, K), BF16), vm((n, 1, pad), F32),
+            vm((n, pad, 128), F32), vm((128, n * pad), BF16), vm((1, n * pad), F32),
+            vm((n, pad // 4, K), BF16), vm((n, 1, pad), F32), vm((n, pad, K), BF16), vm((n, 1, pad), F32),
             vm((n, room, K), BF16), vm((1, W), F32), vm((n, room, K), BF16), vm((n, 1, W), F32),
-            vm((cp, K), F32), vm((n, cp, K), F32),
+            vm((room, K), BF16), vm((n, room, K), BF16),
             vm((LP, IC), F32), vm((n, nc, 2, IC), F32), vm((1, LI), F32), vm((1, LI), F32), vm((LI, W), BF16),
             vm((JT, LI), F32), vm((JT, LI), BF16), vm((JT, 128), F32), vm((JT, 128), F32),
             vm((LP, half), F32), vm((LP, half), F32), vm((LP, half), F32),
             vm((LP, half), BF16), vm((LP, half), BF16),
             vm((4, 1, LP), F32), vm((n, 1, pad), F32), vm((n, 1, pad), F32),
-        ] + [dma((6,)), dma((1,)), dma((n,)), dma((1,)), dma((n,))] + [dma((1,))] * 12
+        ] + [dma((7,)), dma((1,)), dma((n,)), dma((1,)), dma((n,))] + [dma((1,))] * 3 + [dma((2,))] + [dma((1,))] * 8
         + [dma((nc,))] * 2 + [dma((1,)), dma((nt,))] * 3 + [dma((1,))] * 4,
         compiler_params=pltpu.CompilerParams(collective_id=1, has_side_effects=True, vmem_limit_bytes=LIMIT),
-    )(*[pltpu.with_memory_space_constraint(v, pltpu.HBM) for v in (fm, cols, chars, mean, tastes, coef)])
-
-
-def firm_kernel(x, m, srow, home, out, mk, shares):
-    block = m.shape[1]
-    W = x.shape[1]
-    step = pl.program_id(0)
-
-    @pl.when(step == 0)
+    )(*[pltpu.with_memory_space_constraint(v, pltpu.HBM) for v in (fm, cols, chars, mean, tastes, coef, inv)])
+
+
+def firm_kernel(x, pairs, mk, home, out, markup, shares):
+    block = pairs.shape[1]
+    W = out.shape[1]
+
+    @pl.when(pl.program_id(0) == 0)
     def _():
         shares[...] = home[...]
-
-    for b in range(m.shape[0]):
+        markup[...] = mk[...]
+
+    for b in range(pairs.shape[0]):
         rows = slice(b * block, (b + 1) * block)
-        mh = m[b].astype(BF16)
-        pair = jnp.concatenate([mh, (m[b] - mh.astype(F32)).astype(BF16)], axis=1)
-        v = x[rows, :]
-        h = v.astype(BF16)
-        both = jnp.concatenate([h, (v - h.astype(F32)).astype(BF16)], axis=1)
-        r = jnp.dot(pair, jnp.concatenate([both, both], axis=0), preferred_element_type=F32)
+        both = x[rows, :]
+        r = jnp.dot(pairs[b], jnp.concatenate([both, both], axis=0), preferred_element_type=F32)
         out[rows, :] = r[:, :W] + r[:, W:]
-        s = srow[:, rows]
-        s1 = s.astype(BF16).astype(F32)
-        left = jnp.concatenate([jnp.broadcast_to(s1, (8, block)), jnp.broadcast_to(s - s1, (8, block))], axis=0).astype(BF16)
-        g = lax.dot_general(jnp.concatenate([left, left], axis=1), pair, NT, preferred_element_type=F32)
-        mk[pl.ds(step * m.shape[0] + b, 1), :] = g[0:1] + g[8:9]
-
-
-def firms(x, inv, srow, home):
-    LP, W = x.shape
-    block = inv.shape[1]
-    per = min(8, inv.shape[0])
-    steps = inv.shape[0] // per
+
+
+def firms(x, pairs, mk, home):
+    LP, W = x.shape[0], x.shape[1] // 2
+    count, block = pairs.shape[0], pairs.shape[1]
+    per = min(8, count)
+    whole = lambda a: pl.BlockSpec(a.shape, lambda i: (0, 0))
     return pl.pallas_call(
         firm_kernel,
-        grid=(steps,),
+        grid=(count // per,),
         out_shape=(
             jax.ShapeDtypeStruct((LP, W), F32),
-            jax.ShapeDtypeStruct((inv.shape[0], block), F32),
+            jax.ShapeDtypeStruct(mk.shape, F32),
             jax.ShapeDtypeStruct(home.shape, F32),
         ),
         in_specs=[
-            pl.BlockSpec((per * block, W), lambda i: (i, 0)),
-            pl.BlockSpec((per, block, block), lambda i: (i, 0, 0)),
-            pl.BlockSpec((1, per * block), lambda i: (0, i)),
-            pl.BlockSpec(home.shape, lambda i: (0, 0)),
+            pl.BlockSpec((per * block, 2 * W), lambda i: (i, 0)),
+            pl.BlockSpec((per, block, 2 * block), lambda i: (i, 0, 0)),
+            whole(mk),
+            whole(home),
         ],
-        out_specs=(
-            pl.BlockSpec((per * block, W), lambda i: (i, 0)),
-            pl.BlockSpec((inv.shape[0], block), lambda i: (0, 0)),
-            pl.BlockSpec(home.shape, lambda i: (0, 0)),
-        ),
+        out_specs=(pl.BlockSpec((per * block, W), lambda i: (i, 0)), whole(mk), whole(home)),
         compiler_params=pltpu.CompilerParams(vmem_limit_bytes=16 * 1024 * 1024),
-    )(x, inv, srow, home)
+    )(x, pairs, mk, home)
 
 
 def body(tastes, price_coef, characteristics, mean_utility, panel_cols, firm_map, inverses):
     n = lax.axis_size("prod")
     LP = characteristics.shape[0]
-    jacobian, srow, home = run(
+    jacobian, pairs, mk, home = run(
         n, LP * n, tastes.shape[0] * lax.axis_size("cons"),
         firm_map[None, :], panel_cols[None, :], characteristics, mean_utility[None, :],
-        tastes, price_coef[None, :],
+        tastes, price_coef[None, :], inverses,
     )
-    response, markup, shares = firms(jacobian, inverses, srow, home)
+    response, markup, shares = firms(jacobian, pairs, mk, home)
     return shares.reshape(LP), markup.reshape(LP), response
 
 

time: 54.7 us -> 53.6 us (0.980)
  Pallas kernels: 53.9 us -> 52.8 us
    pallas_call x1, Pallas kernels: 51.7 us -> 50.9 us  [run(): pl.pallas_call(functools.partial(step_kernel, n, cp, room, pad, float(cou...]
where the time goes in v4:
time: 53.6 us; the launch traced here: 53.4 us
  Pallas kernels  52.8 us (99%)
  between operations  0.64 us (1%)
    pallas_call x1, Pallas kernels, run(): pl.pallas_call(functools.partial(step_kernel, n, cp, room, pad, float(cou...  50.9 us
    pallas_call x1, Pallas kernels, firms(): pl.pallas_call(firm_kernel, grid=(count // per,), out_shape=(jax.ShapeDty...  1.91 us

profile of v4, /device:TPU:0, one launch (start us, length us, event | category | flops | bytes accessed | tf_op | source)
XLA Modules:
  0.0 53.4 jit_solution(3573895744750656942)
XLA Ops:
  0.6 50.9 %shard_map.94 = (bf16[2048,512]{1,0:T(8,128)(2,1)S(1)}, bf16[16,128,256]{2,1,0:T(8,128)(2,1)S(1)}, f32[16,128]{1,0:T(8,128)S(1)}, f32[16,128]{1,0:T(8,128)S(1)}) custom-call(s32[1,2048]{1,0:T(1,128)} %bitcast.7, s32[1,256]{1,0:T(1,128)} %bitcast.9, bf16[2048,128]{1,0:T(8,128)(2,1)} %chars.1, f32[1,2048]{1,0:T(1,128)} %bitcast.8, bf16[4096,128]{1,0:T(8,128)(2,1)} %tastes.1, ...), custom_call_target="tpu_custom_call" | custom-call | tf_op jit(solution)/shard_map/pallas_call | solution.py:519
  51.5 1.9 %shard_map.95 = (f32[2048,256]{1,0:T(8,128)}, f32[16,128]{1,0:T(8,128)}, f32[16,128]{1,0:T(8,128)}) custom-call(bf16[2048,512]{1,0:T(8,128)(2,1)S(1)} %get-tuple-element.10.x, bf16[16,128,256]{2,1,0:T(8,128)(2,1)S(1)} %get-tuple-element.11.pairs, f32[16,128]{1,0:T(8,128)S(1)} %get-tuple-element.12.mk, f32[16,128]{1,0:T(8,128)S(1)} %get-tuple-element.13.home), custom_call_target="tpu_custom_call" | custom-call | tf_op jit(solution)/shard_map/pallas_call | solution.py:572

commit v5 on v4

--- a/solution.py
+++ b/solution.py
@@ -103,8 +103,16 @@
     load_tastes.start()
     load_inv = pltpu.make_async_copy(inv_in, inv, i_s.at[6])
     load_inv.start()
+
+    TA[:, K:] = jnp.where(lax.broadcasted_iota(jnp.int32, (LI, K), 1) < 3, 1.0, 0.0).astype(BF16)
+    at0 = lax.broadcasted_iota(jnp.int32, (128, 128), 0)
+    at1 = lax.broadcasted_iota(jnp.int32, (128, 128), 1)
+    before = jnp.where(at0 < at1, 1.0, 0.0).astype(BF16)
+    q0 = lax.broadcasted_iota(jnp.int32, (nb * n, nb * n), 0).astype(F32)
+    q1 = lax.broadcasted_iota(jnp.int32, (nb * n, nb * n), 1).astype(F32)
+    b0, b1 = jnp.floor((q0 + 0.5) * (1.0 / n)), jnp.floor((q1 + 0.5) * (1.0 / n))
+    earlier = jnp.where((q0 - b0 * n == q1 - b1 * n) & (b1 < b0), 1.0, 0.0).astype(BF16)
     small[0].wait()
-
     fmf = fm[...].astype(F32)
     source = jnp.floor((fmf + 0.5) * (1.0 / LP))
     local = fmf - source * float(LP)
@@ -112,15 +120,8 @@
     marks = jnp.concatenate(
         [jnp.where(source[:, b * 128:(b + 1) * 128] == owners, 1.0, 0.0) for b in range(nb)], axis=0
     )
-    at0 = lax.broadcasted_iota(jnp.int32, (128, 128), 0)
-    at1 = lax.broadcasted_iota(jnp.int32, (128, 128), 1)
-    before = jnp.where(at0 < at1, 1.0, 0.0).astype(BF16)
     inner = jnp.dot(marks.astype(BF16), before, preferred_element_type=F32)
     totals = jnp.dot(marks.astype(BF16), jnp.ones((128, 128), BF16), preferred_element_type=F32)
-    q0 = lax.broadcasted_iota(jnp.int32, (nb * n, nb * n), 0).astype(F32)
-    q1 = lax.broadcasted_iota(jnp.int32, (nb * n, nb * n), 1).astype(F32)
-    b0, b1 = jnp.floor((q0 + 0.5) * (1.0 / n)), jnp.floor((q1 + 0.5) * (1.0 / n))
-    earlier = jnp.where((q0 - b0 * n == q1 - b1 * n) & (b1 < b0), 1.0, 0.0).astype(BF16)
     offset = jnp.dot(earlier, totals.astype(BF16), preferred_element_type=F32)
     placed = marks * (inner + offset)
     slot = jnp.concatenate(
@@ -149,7 +150,6 @@
     small[1].wait()
     for g in range(nb):
         CA[g * 128:(g + 1) * 128, K:] = split(turned(mean[:, g * 128:(g + 1) * 128]), K)
-    TA[:, K:] = jnp.where(lax.broadcasted_iota(jnp.int32, (LI, K), 1) < 3, 1.0, 0.0).astype(BF16)
     pl.semaphore_wait(barrier, n + 2)
 
     def a_copy(d):
@@ -380,7 +380,7 @@
 
     def o_copy(jt, k):
         rows = tile_rows(jt)
-        return to_cons(out.at[rows, mine[k]], out.at[rows, mine[k]], o_s.at[0], o_r.at[jt], partner)
+        return to_cons(out.at[rows, mine[k]], out.at[rows, mine[k]], o_s.at[0], o_r.at[0], partner)
 
     def st_copy(d, jt):
         rows = tile_rows(jt)
@@ -403,10 +403,6 @@
         out[rows, mine[1]] = (x - h.astype(F32)).astype(BF16)
         o_copy(jt, 0).start()
         o_copy(jt, 1).start()
-
-    def gather(jt):
-        both = out.at[tile_rows(jt), pl.ds(0, W)]
-        to_cons(both, both, o_s.at[0], o_r.at[jt], partner).wait_recv()
 
     heads_row = cols[...].astype(F32)
 
@@ -451,10 +447,6 @@
         def _():
             finish(jt - 4)
 
-        @pl.when(jt > 4)
-        def _():
-            gather(jt - 5)
-
         return carry
 
     lax.fori_loop(0, nt, panel, 0)
@@ -488,8 +480,6 @@
         mk[b:b + 1, :] = g[0:1] + g[8:9]
     for t in range(max(nt - 4, 0), nt):
         finish(t)
-    for t in range(max(nt - 5, 0), nt):
-        gather(t)
     all_of(HV.at[rest], h_s.at[0], h_r.at[0]).wait()
     back = jnp.concatenate([HV[p] for p in range(n)], axis=1)
     mask = UP[...] == rows_of((nb, n * pad))
@@ -498,7 +488,7 @@
     home[...] = got[:nb] + (got[nb:2 * nb] + got[2 * nb:])
     to_cons(PX, PR, px_s.at[0], px_r.at[0], partner).wait_send()
     to_cons(YS, YR, y_s.at[0], y_r.at[0], across).wait_send()
-    to_cons(out.at[:, pl.ds(0, W)], out.at[:, pl.ds(0, W)], o_s.at[0], o_r.at[0], partner).wait_send()
+    to_cons(out.at[:, pl.ds(0, W)], out.at[:, pl.ds(0, W)], o_s.at[0], o_r.at[0], partner).wait()
 
 
 def run(n, count_products, count_consumers, fm, cols, chars, mean, tastes, coef, inv):
@@ -543,7 +533,7 @@
             vm((LP, half), BF16), vm((LP, half), BF16),
             vm((4, 1, LP), F32), vm((n, 1, pad), F32), vm((n, 1, pad), F32),
         ] + [dma((7,)), dma((1,)), dma((n,)), dma((1,)), dma((n,))] + [dma((1,))] * 3 + [dma((2,))] + [dma((1,))] * 8
-        + [dma((nc,))] * 2 + [dma((1,)), dma((nt,))] * 3 + [dma((1,))] * 4,
+        + [dma((nc,))] * 2 + [dma((1,)), dma((nt,))] * 2 + [dma((1,))] * 6,
         compiler_params=pltpu.CompilerParams(collective_id=1, has_side_effects=True, vmem_limit_bytes=LIMIT),
     )(*[pltpu.with_memory_space_constraint(v, pltpu.HBM) for v in (fm, cols, chars, mean, tastes, coef, inv)])
 
@@ -557,10 +547,12 @@
         shares[...] = home[...]
         markup[...] = mk[...]
 
-    for b in range(pairs.shape[0]):
+    per = out.shape[0] // block
+    for b in range(per):
         rows = slice(b * block, (b + 1) * block)
-        both = x[rows, :]
-        r = jnp.dot(pairs[b], jnp.concatenate([both, both], axis=0), preferred_element_type=F32)
+        at = pl.program_id(0) * per + b
+        both = x[pl.ds(pl.multiple_of(at * block, block), block), :]
+        r = jnp.dot(pairs[at], jnp.concatenate([both, both], axis=0), preferred_element_type=F32)
         out[rows, :] = r[:, :W] + r[:, W:]
 
 
@@ -578,8 +570,8 @@
             jax.ShapeDtypeStruct(home.shape, F32),
         ),
         in_specs=[
-            pl.BlockSpec((per * block, 2 * W), lambda i: (i, 0)),
-            pl.BlockSpec((per, block, 2 * block), lambda i: (i, 0, 0)),
+            VMEM,
+            VMEM,
             whole(mk),
             whole(home),
         ],

time: 53.6 us -> 53.5 us (level)
  no operation moved by 1% of the time
where the time goes in v5:
time: 53.5 us; the launch traced here: 53.3 us
  Pallas kernels  52.7 us (99%)
  between operations  0.64 us (1%)
    pallas_call x1, Pallas kernels, run(): pl.pallas_call(functools.partial(step_kernel, n, cp, room, pad, float(cou...  50.8 us
    pallas_call x1, Pallas kernels, firms(): pl.pallas_call(firm_kernel, grid=(count // per,), out_shape=(jax.ShapeDty...  1.91 us

profile of v5, /device:TPU:0, one launch (start us, length us, event | category | flops | bytes accessed | tf_op | source)
XLA Modules:
  0.0 53.3 jit_solution(16007411052573495414)
XLA Ops:
  0.6 50.8 %shard_map.94 = (bf16[2048,512]{1,0:T(8,128)(2,1)S(1)}, bf16[16,128,256]{2,1,0:T(8,128)(2,1)S(1)}, f32[16,128]{1,0:T(8,128)S(1)}, f32[16,128]{1,0:T(8,128)S(1)}) custom-call(s32[1,2048]{1,0:T(1,128)} %bitcast.7, s32[1,256]{1,0:T(1,128)} %bitcast.9, bf16[2048,128]{1,0:T(8,128)(2,1)} %chars.1, f32[1,2048]{1,0:T(1,128)} %bitcast.8, bf16[4096,128]{1,0:T(8,128)(2,1)} %tastes.1, ...), custom_call_target="tpu_custom_call" | custom-call | tf_op jit(solution)/shard_map/pallas_call | solution.py:509
  51.4 1.9 %shard_map.95 = (f32[2048,256]{1,0:T(8,128)}, f32[16,128]{1,0:T(8,128)}, f32[16,128]{1,0:T(8,128)}) custom-call(bf16[2048,512]{1,0:T(8,128)(2,1)S(1)} %get-tuple-element.10.x, bf16[16,128,256]{2,1,0:T(8,128)(2,1)S(1)} %get-tuple-element.11.pairs, f32[16,128]{1,0:T(8,128)S(1)} %get-tuple-element.12.mk, f32[16,128]{1,0:T(8,128)S(1)} %get-tuple-element.13.home), custom_call_target="tpu_custom_call" | custom-call | tf_op jit(solution)/shard_map/pallas_call | solution.py:564

commit v6 on v5

--- a/solution.py
+++ b/solution.py
@@ -244,11 +244,10 @@
             [jnp.where(want == spot + float(b * 128), 1.0, 0.0).astype(BF16) for b in range(nb)], axis=1
         )
 
-    asks = jnp.concatenate([hots(IDC[p, part, :]) for p in range(n)] + [hots(IDC[me])], axis=0)
+    asks = jnp.concatenate([hots(IDC[p, part, :]) for p in range(n)], axis=0)
     got = jnp.dot(asks, CA[:, :K], preferred_element_type=F32).astype(BF16)
     for p in range(n):
         X[p] = got[p * span:(p + 1) * span]
-    R[me] = got[n * span:]
     loop(lambda d: x_copy(d).start())
     idf = (jnp.concatenate([asked[p] for p in range(n)], axis=1) - base).astype(F32)
     up = jnp.floor((idf + 0.5) * (1.0 / 128))
@@ -272,6 +271,7 @@
     CP[:cp, :] = total.astype(BF16)
     loop(lambda d: cc_copy(d).start())
     CC[me] = CP[...]
+    R[me] = jnp.dot(hots(IDC[me]), CA[:, :K], preferred_element_type=F32).astype(BF16)
 
     RM[me] = XM[me]
     held = max(nc - 1, 1)

time: 53.5 us -> 53 us (level)
  no operation moved by 1% of the time
where the time goes in v6:
time: 53 us; the launch traced here: 52.8 us
  Pallas kernels  52.2 us (98%)
  between operations  0.64 us (1%)
    pallas_call x1, Pallas kernels, run(): pl.pallas_call(functools.partial(step_kernel, n, cp, room, pad, float(cou...  50.2 us
    pallas_call x1, Pallas kernels, firms(): pl.pallas_call(firm_kernel, grid=(count // per,), out_shape=(jax.ShapeDty...  1.91 us

profile of v6, /device:TPU:0, one launch (start us, length us, event | category | flops | bytes accessed | tf_op | source)
XLA Modules:
  0.0 52.8 jit_solution(4261624846810587752)
XLA Ops:
  0.6 50.2 %shard_map.94 = (bf16[2048,512]{1,0:T(8,128)(2,1)S(1)}, bf16[16,128,256]{2,1,0:T(8,128)(2,1)S(1)}, f32[16,128]{1,0:T(8,128)S(1)}, f32[16,128]{1,0:T(8,128)S(1)}) custom-call(s32[1,2048]{1,0:T(1,128)} %bitcast.7, s32[1,256]{1,0:T(1,128)} %bitcast.9, bf16[2048,128]{1,0:T(8,128)(2,1)} %chars.1, f32[1,2048]{1,0:T(1,128)} %bitcast.8, bf16[4096,128]{1,0:T(8,128)(2,1)} %tastes.1, ...), custom_call_target="tpu_custom_call" | custom-call | tf_op jit(solution)/shard_map/pallas_call | solution.py:509
  50.9 1.9 %shard_map.95 = (f32[2048,256]{1,0:T(8,128)}, f32[16,128]{1,0:T(8,128)}, f32[16,128]{1,0:T(8,128)}) custom-call(bf16[2048,512]{1,0:T(8,128)(2,1)S(1)} %get-tuple-element.10.x, bf16[16,128,256]{2,1,0:T(8,128)(2,1)S(1)} %get-tuple-element.11.pairs, f32[16,128]{1,0:T(8,128)S(1)} %get-tuple-element.12.mk, f32[16,128]{1,0:T(8,128)S(1)} %get-tuple-element.13.home), custom_call_target="tpu_custom_call" | custom-call | tf_op jit(solution)/shard_map/pallas_call | solution.py:564
